TPU v7x, 32 devices: a whole 2x2x4 slice. The times are simulated.
32 devices in a mesh: grp: 2 (over y), seq: 8 (over z, x), tp: 2 (over core).
Axes of the slice: x: 2, y: 2, z: 4, core: 2. Of those that a mesh axis runs over, the one named last changes fastest.
Arguments:
- hidden: bfloat16 [8, 8192], P('grp', 'seq'), parts along dimension 0, may hold values from -40 to 40
- norm_gain: float32 [8192], P('seq'), may hold values from 0.25 to 1.75
- query_proj: bfloat16 [8192, 4096], P('seq', 'tp'), may hold values from -0.0625 to 0.0625
- keyval_proj: bfloat16 [8192, 2, 512], P('seq', None, 'tp'), may hold values from -0.0625 to 0.0625
- attend_proj: bfloat16 [4096, 8192], P('tp', 'seq'), may hold values from -0.09375 to 0.09375
- keyval_cache: bfloat16 [2, 8, 512, 512], P(None, 'grp', 'seq', 'tp'), parts along dimension 1, may hold values from -320 to 320
- lengths: int32 [8], P('grp'), parts along dimension 0, may hold values from 1 to 512, as said below
Outputs:
- hidden_out: bfloat16 [8, 8192], P('grp', 'seq'), parts along dimension 0
- new_keyval: bfloat16 [8, 2, 512], P('grp', None, 'tp'), parts along dimension 0
There are 2 independent parts, one for each index of `grp`. A program takes and returns all parts, laid end to end along the dimension named above; an argument that names none is the same for every part. Nothing has to cross between parts.
Inputs may be any that keep to these rules, and one draw needn't show every extreme that they name: `lengths`: live cached positions of each request; in every draw some request has all 512.
All inputs are finite; a program needn't handle non-finite values.
Results may differ from a plain program's by a relative error of at most 0.0087.
Values sent between devices are 32-bit elements; how exact they have to be, the bound alone decides.
No kernel may reach another device: no remote copies, remote signals or barrier semaphores. Data moves between devices by JAX's collectives and lax.ppermute only.
A program may use at most 64 MiB of HBM per device.

v0:
```python
import jax
import jax.numpy as jnp
from jax import lax
from jax.sharding import PartitionSpec as P

D = 8192
HEAD_DIM = 128


EPSILON = 1e-05
MASKED = -1e30


def on_device(hidden, norm_gain, query_proj, keyval_proj, attend_proj, keyval_cache, lengths):
    row_count = hidden.shape[0]
    feature_dev = hidden.shape[1]
    seq_rank = lax.axis_index("seq")
    ctx_dev = keyval_cache.shape[2]
    kv_width = keyval_cache.shape[3]
    kv_heads = kv_width // HEAD_DIM
    q_heads = query_proj.shape[1] // HEAD_DIM
    group_share = q_heads // kv_heads
    score_scale = HEAD_DIM ** (-0.5)
    one_float = hidden.astype(jnp.float32)
    scaled = (one_float * norm_gain).astype(jnp.bfloat16)
    squares = jnp.sum(one_float * one_float, axis=1)
    query_part = jnp.dot(scaled, query_proj, preferred_element_type=jnp.float32)
    keyval_part = jnp.dot(
        scaled, keyval_proj.reshape(feature_dev, 2 * kv_width), preferred_element_type=jnp.float32
    ).reshape(row_count, 2, kv_width)
    query_sum, keyval_sum, squares_sum = lax.psum((query_part, keyval_part, squares), "seq")
    scale_two = lax.rsqrt(squares_sum / D + EPSILON)[:, None]
    query = (query_sum * scale_two).astype(jnp.bfloat16)
    new_keyval = (keyval_sum * scale_two[:, :, None]).astype(jnp.bfloat16)
    query_heads = query.reshape(row_count, kv_heads, group_share, HEAD_DIM)
    cache_keys = keyval_cache[0].reshape(row_count, ctx_dev, kv_heads, HEAD_DIM)
    cache_values = keyval_cache[1].reshape(row_count, ctx_dev, kv_heads, HEAD_DIM)
    scores = (
        jnp.einsum("rkgd,rskd->rkgs", query_heads, cache_keys, preferred_element_type=jnp.float32)
        * score_scale
    )
    positions = seq_rank * ctx_dev + jnp.arange(ctx_dev, dtype=jnp.int32)
    live_mask = (positions[None, :] < lengths[:, None])[:, None, None, :]
    scores = jnp.where(live_mask, scores, MASKED)
    block_max = jnp.max(scores, axis=3)
    weights = jnp.where(live_mask, jnp.exp(scores - block_max[..., None]), 0.0).astype(jnp.bfloat16)
    block_total = jnp.sum(lax.optimization_barrier(weights).astype(jnp.float32), axis=3)
    block_out = jnp.einsum(
        "rkgs,rskd->rkgd", weights, cache_values, preferred_element_type=jnp.float32
    )
    best_score = lax.pmax(block_max, "seq")
    factor = jnp.exp(block_max - best_score)
    total_weight, gathered = lax.psum((block_total * factor, block_out * factor[..., None]), "seq")
    own_key = new_keyval[:, 0].reshape(row_count, kv_heads, HEAD_DIM)
    own_value = new_keyval[:, 1].reshape(row_count, kv_heads, HEAD_DIM).astype(jnp.float32)
    own_score = (
        jnp.einsum("rkgd,rkd->rkg", query_heads, own_key, preferred_element_type=jnp.float32)
        * score_scale
    )
    top_score = jnp.maximum(best_score, own_score)
    old_weight = jnp.exp(best_score - top_score)
    fresh_weight = jnp.exp(own_score - top_score)
    attended = (
        old_weight[..., None] * gathered + fresh_weight[..., None] * own_value[:, :, None, :]
    ) / (old_weight * total_weight + fresh_weight)[..., None]
    attended = attended.reshape(row_count, q_heads * HEAD_DIM).astype(jnp.bfloat16)
    attend_term = jnp.dot(attended, attend_proj, preferred_element_type=jnp.float32)
    hidden_out = (one_float + lax.psum(attend_term, "tp")).astype(jnp.bfloat16)
    return (hidden_out, new_keyval)


def solution(mesh):
    in_specs = (
        P("grp", "seq"),
        P("seq"),
        P("seq", "tp"),
        P("seq", None, "tp"),
        P("tp", "seq"),
        P(None, "grp", "seq", "tp"),
        P("grp"),
    )
    out_specs = (P("grp", "seq"), P("grp", None, "tp"))
    return jax.shard_map(
        on_device, mesh=mesh, in_specs=in_specs, out_specs=out_specs, check_vma=False
    )
```

profile of v0, /device:TPU:0, one launch (start us, length us, event | category | flops | bytes accessed | tf_op | source)
XLA Modules:
  0.0 106.3 jit_solution(10798045610524827243)
XLA Ops:
  0.6 0.0 copy-start.1
  0.6 0.0 copy-start.2
  0.7 0.0 copy-start
  0.7 1.5 %copy.18 = bf16[128,8,2,256]{3,1,2,0:T(8,128)(2,1)S(1)} copy(bf16[128,8,2,256]{3,2,1,0:T(2,128)(2,1)} %bitcast.46) | data formatting | bytes 2097152
  2.2 0.0 copy-start.3
  2.2 0.5 copy.12
  2.7 0.0 copy-done.1
  2.7 0.0 copy-done.2
  2.7 0.4 fusion.16
  3.1 0.0 copy-done
  3.2 2.8 %fusion.19 = f32[4,2048]{1,0:T(4,128)S(1)} fusion(bf16[1024,2048]{1,0:T(8,128)(2,1)} %param.9, bf16[4,1024]{1,0:T(4,128)(2,1)S(1)} %copy-done.1, f32[1024]{0:T(1024)S(1)} %copy-done.2), kind=kOutput, calls=%fused_computation.30 | convolution fusion | flops 16789504 | bytes 4239360 | tf_op jit(solution)/shard_map/dot_general | solution.py:27
  6.0 0.1 fusion.4
  6.2 39.2 %all-reduce.1 = (f32[4,2048]{1,0:T(4,128)S(1)}, f32[4]{0:T(128)S(1)}) all-reduce(f32[4,2048]{1,0:T(4,128)S(1)} %fusion.19, f32[4]{0:T(128)S(1)} %fusion.4), channel_id=1, replica_groups=mesh['grp'=2,'seq'=8,'tp'=2] {'seq'}, use_global_device_ids=true, to_apply=%region_0.0 | all-reduce | flops 8196 | bytes 65568 | tf_op jit(solution)/shard_map/psum | solution.py:31
  45.3 0.1 fusion.6
  45.4 0.0 copy-done.3
  45.4 0.1 broadcast_compare_fusion
  45.5 0.2 fusion.27
  45.7 0.1 select_convert_fusion
  45.9 0.1 convert_reduce_fusion
  46.0 17.1 %pmax.7 = f32[4,2,8]{2,1,0:T(2,128)S(1)} all-reduce(f32[4,2,8]{2,1,0:T(2,128)S(1)} %get-tuple-element.20), channel_id=1, replica_groups=mesh['grp'=2,'seq'=8,'tp'=2] {'seq'}, use_global_device_ids=true, to_apply=%region_4.5 | all-reduce | flops 64 | bytes 512 | tf_op jit(solution)/shard_map/pmax | solution.py:51
  63.1 0.1 convolution_multiply_fusion
  63.2 35.3 %all-reduce = (f32[4,2,256]{2,0,1:T(4,128)S(1)}, f32[4,2,8]{2,1,0:T(2,128)S(1)}, f32[4,2,8,128]{3,2,1,0:T(8,128)S(1)}) all-reduce(f32[4,2,256]{2,0,1:T(4,128)S(1)} %fusion.16, f32[4,2,8]{2,1,0:T(2,128)S(1)} %bitcast.50, f32[4,2,8,128]{3,2,1,0:T(8,128)S(1)} %convolution_multiply_fusion), channel_id=1, replica_groups=mesh['grp'=2,'seq'=8,'tp'=2] {'seq'}, use_global_device_ids=true, to_apply=%region_5.6 | all-reduce | flops 10304 | bytes 82432 | tf_op jit(solution)/shard_map/psum | solution.py:31
  98.5 0.1 multiply_convert_fusion.1
  98.6 0.1 fusion.10
  98.8 0.1 fusion.13
  98.9 2.8 %fusion.7 = f32[4,1024]{1,0:T(4,128)S(1)} fusion(bf16[2048,1024]{1,0:T(8,128)(2,1)} %param.11, bf16[1,4,16,128]{3,2,1,0:T(8,128)(2,1)S(1)} %fusion.13), kind=kOutput, calls=%fused_computation.16 | convolution fusion | flops 16777216 | bytes 4227072 | tf_op jit(solution)/shard_map/dot_general | solution.py:67
  101.7 3.4 %psum.47 = f32[4,1024]{1,0:T(4,128)S(1)} all-reduce(f32[4,1024]{1,0:T(4,128)S(1)} %fusion.7), channel_id=1, replica_groups=mesh['grp'=2,'seq'=8,'tp'=2] {'tp'}, use_global_device_ids=true, to_apply=%region_9.10 | all-reduce | flops 4096 | bytes 32768 | tf_op jit(solution)/shard_map/psum | solution.py:68
  105.1 0.6 fusion.5
  105.7 0.6 copy.14
  (10 shorter events, 0.2 us)
Async XLA Ops:
  0.6 2.1 %copy-start.1 = (bf16[4,1024]{1,0:T(4,128)(2,1)S(1)}, bf16[4,1024]{1,0:T(4,128)(2,1)}, u32[]{:S(2)}) copy-start(bf16[4,1024]{1,0:T(4,128)(2,1)} %param.7) | copy-start | bytes 24580
  0.6 2.1 %copy-start.2 = (f32[1024]{0:T(1024)S(1)}, f32[1024]{0:T(1024)}, u32[]{:S(2)}) copy-start(f32[1024]{0:T(1024)} %param.8) | copy-start | bytes 12292
  0.7 2.5 %copy-start = (bf16[2,4,64,256]{3,2,1,0:T(8,128)(2,1)S(1)}, bf16[2,4,64,256]{3,2,1,0:T(8,128)(2,1)}, u32[]{:S(2)}) copy-start(bf16[2,4,64,256]{3,2,1,0:T(8,128)(2,1)} %param.12) | copy-start | bytes 786436
  2.2 43.3 %copy-start.3 = (s32[4]{0:T(128)S(1)}, s32[4]{0:T(128)}, u32[]{:S(2)}) copy-start(s32[4]{0:T(128)} %param.13) | copy-start | bytes 52
where the time goes:
time: 107 us; the launch traced here: 106 us
  blocking collectives  94.9 us (89%)
  matrix products  6.52 us (6%)
  local copies, waits for them, and re-layouts  2.77 us (3%)
  other arithmetic  1.3 us (1%)
    psum x2, blocking collectives, on_device(): lax.psum((query_part, keyval_part, squares), 'seq')  74.5 us
    pmax x1, blocking collectives, on_device(): best_score = lax.pmax(block_max, 'seq')  17.1 us
    psum x1, blocking collectives, on_device(): hidden_out = (one_float + lax.psum(attend_term, 'tp')).astype(jnp.bfloat16)  3.35 us
    dot_general x1, matrix products, on_device(): query_part = jnp.dot(scaled, query_proj, preferred_element_type=jnp.float32)  2.84 us
    dot_general x1, matrix products, on_device(): jnp.dot(attended, attend_proj, preferred_element_type=jnp.float32)  2.84 us

commit v1 on v0

v1 whole, which is shorter than its diff:
```python
import functools

import jax
import jax.numpy as jnp
from jax import lax
from jax.experimental import pallas as pl
from jax.experimental.pallas import tpu as pltpu
from jax.sharding import PartitionSpec as P


HEAD_DIM = 128

EPSILON = 1e-05
MASKED = -1e30


COVER = 16 << 20
COVER_OPS = 1 << 30

VMEM = pl.BlockSpec(memory_space=pltpu.VMEM)
SMEM = pl.BlockSpec(memory_space=pltpu.SMEM)


def call(kernel, outs, ins, flops, bytes_accessed, other_ops=0):
    return pl.pallas_call(
        kernel,
        out_shape=outs,
        in_specs=[SMEM if a.dtype == jnp.int32 else VMEM for a in ins],
        out_specs=[VMEM] * len(outs),
        compiler_params=pltpu.CompilerParams(vmem_limit_bytes=16 << 20),
        cost_estimate=pl.CostEstimate(
            flops=flops, bytes_accessed=bytes_accessed, transcendentals=other_ops
        ),
    )(*ins)


def stages(size):
    bits = size.bit_length() - 1
    out = []
    bit = 1
    while bit < bits:
        if bit + 1 < bits:
            out.append((2 << bit, 3 << bit, 1 << bit))
            bit += 2
        else:
            out.append((1 << bit,))
            bit += 1
    return out


def partners(value, axis, size, offsets):
    got = []
    for offset in offsets:
        got.append(lax.ppermute(value, axis, [(i, i ^ offset) for i in range(size)]))
    return got


def widen_kernel(cache_ref, out_ref):
    out_ref[...] = cache_ref[...].astype(jnp.float32)


def query_kernel(hidden_ref, gain_ref, proj_ref, out_ref):
    width = proj_ref.shape[1]
    one_float = hidden_ref[...].astype(jnp.float32)
    scaled = (one_float * gain_ref[...]).astype(jnp.bfloat16)
    squares = jnp.sum(one_float * one_float, axis=1, keepdims=True)
    out_ref[:, width:] = jnp.broadcast_to(squares, (out_ref.shape[0], HEAD_DIM))
    out_ref[:, :width] = jnp.dot(scaled, proj_ref[...], preferred_element_type=jnp.float32)


def attend_kernel(
    features, width, lengths_ref, mine_ref, other_ref, near_ref, far_ref,
    packed_ref, query_ref, scale_ref,
):
    rows = mine_ref.shape[0]
    heads = width // HEAD_DIM
    ctx = near_ref.shape[2]
    kv_heads = near_ref.shape[3] // HEAD_DIM
    share = heads // kv_heads * rows
    split = heads * rows
    scale = lax.rsqrt(
        (mine_ref[:, width : width + HEAD_DIM] + other_ref[:, width : width + HEAD_DIM])
        / features
        + EPSILON
    )
    scale_ref[...] = scale
    query = jnp.concatenate(
        [
            (mine_ref[:, c : c + HEAD_DIM] + other_ref[:, c : c + HEAD_DIM]) * scale
            for c in range(0, width, HEAD_DIM)
        ],
        axis=0,
    ).astype(jnp.bfloat16)
    query_ref[...] = query
    request = lax.broadcasted_iota(jnp.int32, (split, 2 * ctx), 0) % rows
    lane = lax.broadcasted_iota(jnp.int32, (split, 2 * ctx), 1)
    near = lane < ctx
    length = jnp.zeros((split, 2 * ctx), jnp.int32)
    for r in range(rows):
        length = jnp.where(request == r, lengths_ref[r], length)
    rank = lax.axis_index("seq")
    pair = rank + 1 - 2 * (rank % 2)
    position = jnp.where(near, rank * ctx + lane, pair * ctx + lane - ctx)
    live = position < length

    def blocks(kind, k):
        cut = slice(k * HEAD_DIM, (k + 1) * HEAD_DIM)
        return jnp.concatenate(
            [
                ref[kind, r, :, cut].astype(jnp.bfloat16)
                for r in range(rows)
                for ref in (near_ref, far_ref)
            ],
            axis=0,
        )

    scores = []
    for k in range(kv_heads):
        all_scores = lax.dot_general(
            query[k * share : (k + 1) * share],
            blocks(0, k),
            (((1,), (1,)), ((), ())),
            preferred_element_type=jnp.float32,
        )
        own = all_scores[:, : 2 * ctx]
        for r in range(1, rows):
            own = jnp.where(
                request[:share] == r, all_scores[:, 2 * ctx * r : 2 * ctx * (r + 1)], own
            )
        scores.append(own)
    scores = jnp.concatenate(scores, axis=0) * (HEAD_DIM ** (-0.5))
    best = [
        jnp.max(jnp.where(live & side, scores, MASKED), axis=1, keepdims=True)
        for side in (near, ~near)
    ]
    weights = jnp.where(live, jnp.exp(scores - jnp.where(near, best[0], best[1])), 0.0)
    weights = weights.astype(jnp.bfloat16).astype(jnp.float32)
    sides = [jnp.where(side, weights, 0.0) for side in (near, ~near)]
    top = jnp.maximum(best[0], best[1])
    factors = [jnp.exp(b - top) for b in best]
    total = sum(f * jnp.sum(s, axis=1, keepdims=True) for f, s in zip(factors, sides))
    for k in range(kv_heads):
        cut = slice(k * share, (k + 1) * share)
        spread = jnp.concatenate(
            [
                jnp.concatenate(
                    [jnp.where(request[cut] == r, s[cut], 0.0) for r in range(rows)], axis=1
                )
                for s in sides
            ],
            axis=0,
        ).astype(jnp.bfloat16)
        outs = jnp.dot(spread, blocks(1, k), preferred_element_type=jnp.float32)
        packed_ref[cut, :] = factors[0][cut] * outs[:share] + factors[1][cut] * outs[share:]
    column = lax.broadcasted_iota(jnp.int32, (split, HEAD_DIM), 1)
    pair = jnp.where(column == 0, top, jnp.where(column == 1, total, 0.0))
    pair = jnp.concatenate([pair, jnp.zeros((HEAD_DIM - split, HEAD_DIM), jnp.float32)], axis=0)
    packed_ref[split : split + 8, :] = jnp.transpose(pair)[:8]
    for j in range(2 * kv_heads):
        at = width + HEAD_DIM + j * HEAD_DIM
        packed_ref[split + 8 + rows * j : split + 8 + rows * (j + 1), :] = (
            mine_ref[:, at : at + HEAD_DIM] + other_ref[:, at : at + HEAD_DIM]
        )


def unpack(packed, split):
    pair = jnp.transpose(packed[split : split + 8])
    return packed[:split], pair[:split, 0:1], pair[:split, 1:2], packed[split + 8 :]


def merge(parts):
    best = functools.reduce(jnp.maximum, [p[1] for p in parts])
    factors = [jnp.exp(p[1] - best) for p in parts]
    gathered = sum(f * p[0] for f, p in zip(factors, parts))
    total = sum(f * p[2] for f, p in zip(factors, parts))
    return gathered, best, total, sum(p[3] for p in parts)


def merge_kernel(split, *refs):
    gathered, best, total, keyval = merge([unpack(ref[...], split) for ref in refs[:-1]])
    packed_ref = refs[-1]
    packed_ref[:split, :] = gathered
    column = lax.broadcasted_iota(jnp.int32, (split, HEAD_DIM), 1)
    pair = jnp.where(column == 0, best, jnp.where(column == 1, total, 0.0))
    pair = jnp.concatenate([pair, jnp.zeros((HEAD_DIM - split, HEAD_DIM), jnp.float32)], axis=0)
    packed_ref[split : split + 8, :] = jnp.transpose(pair)[:8]
    packed_ref[split + 8 :, :] = keyval


def output_kernel(parts, query_ref, scale_ref, proj_ref, *refs):
    packed, (out_ref, new_ref) = refs[:parts], refs[parts:]
    split = query_ref.shape[0]
    rows = scale_ref.shape[0]
    gathered, best, total, keyval = merge([unpack(ref[...], split) for ref in packed])
    kv_heads = keyval.shape[0] // rows // 2
    group = split // rows // kv_heads
    new = (keyval * jnp.concatenate([scale_ref[...]] * (2 * kv_heads), axis=0)).astype(jnp.bfloat16)
    new = new.astype(jnp.float32)
    for j in range(2 * kv_heads):
        new_ref[:, j * HEAD_DIM : (j + 1) * HEAD_DIM] = new[j * rows : (j + 1) * rows]
    own_key, own_value = (
        jnp.concatenate(
            [
                new[(kind * kv_heads + k) * rows : (kind * kv_heads + k + 1) * rows]
                for k in range(kv_heads)
                for _ in range(group)
            ],
            axis=0,
        )
        for kind in range(2)
    )
    query = query_ref[...].astype(jnp.float32)
    own_score = jnp.sum(query * own_key, axis=1, keepdims=True) * (HEAD_DIM ** (-0.5))
    top = jnp.maximum(best, own_score)
    old_weight = jnp.exp(best - top)
    fresh_weight = jnp.exp(own_score - top)
    attended = (old_weight * gathered + fresh_weight * own_value) / (
        old_weight * total + fresh_weight
    )
    attended = jnp.concatenate(
        [attended[r : r + rows] for r in range(0, split, rows)], axis=1
    ).astype(jnp.bfloat16)
    out_ref[...] = jnp.dot(attended, proj_ref[...], preferred_element_type=jnp.float32)


def on_device(
    seq, tp, hidden, norm_gain, query_proj, keyval_proj, attend_proj, keyval_cache, lengths
):
    f32 = jnp.float32
    rows, feature_dev = hidden.shape
    kv_width = keyval_cache.shape[3]
    width = query_proj.shape[1]
    split = rows * width // HEAD_DIM
    one_float = hidden.astype(f32)

    near = call(
        widen_kernel,
        [jax.ShapeDtypeStruct(keyval_cache.shape, f32)],
        [keyval_cache],
        0,
        COVER,
        COVER_OPS,
    )[0]
    far = partners(near, "seq", seq, (1,))[0]

    first = call(
        query_kernel,
        [jax.ShapeDtypeStruct((rows, width + HEAD_DIM), f32)],
        [hidden, norm_gain.reshape(1, feature_dev), query_proj],
        2 * rows * feature_dev * width,
        COVER,
    )[0]
    for offsets in stages(seq):
        for other in partners(first, "seq", seq, offsets):
            first = first + other
    scaled = (one_float * norm_gain).astype(jnp.bfloat16)
    keyval_part = jnp.dot(
        scaled, keyval_proj.reshape(feature_dev, 2 * kv_width), preferred_element_type=f32
    )
    first = jnp.concatenate([first, keyval_part], axis=1)
    second = partners(first, "seq", seq, (1,))[0]

    pack = jax.ShapeDtypeStruct((split + 8 + rows * 2 * kv_width // HEAD_DIM, HEAD_DIM), f32)
    packed, query, scale = call(
        functools.partial(attend_kernel, float(seq * feature_dev), width),
        [
            pack,
            jax.ShapeDtypeStruct((split, HEAD_DIM), jnp.bfloat16),
            jax.ShapeDtypeStruct((rows, HEAD_DIM), f32),
        ],
        [lengths, first, second, near, far],
        16 * split * keyval_cache.shape[2] * HEAD_DIM,
        COVER,
    )
    todo = stages(seq)
    for place, offsets in enumerate(todo):
        parts = [packed] + partners(packed, "seq", seq, offsets)
        if place < len(todo) - 1:
            packed = call(functools.partial(merge_kernel, split), [pack], parts, 0, COVER)[0]
    term, new_keyval = call(
        functools.partial(output_kernel, len(parts)),
        [
            jax.ShapeDtypeStruct((rows, attend_proj.shape[1]), f32),
            jax.ShapeDtypeStruct((rows, 2 * kv_width), f32),
        ],
        [query, scale, attend_proj, *parts],
        2 * rows * width * attend_proj.shape[1],
        COVER,
    )
    for bit in range(tp.bit_length() - 1):
        term = term + partners(term, "tp", tp, (1 << bit,))[0]
    hidden_out = (one_float + term).astype(jnp.bfloat16)
    return (hidden_out, new_keyval.astype(jnp.bfloat16).reshape(rows, 2, kv_width))


def solution(mesh):
    in_specs = (
        P("grp", "seq"),
        P("seq"),
        P("seq", "tp"),
        P("seq", None, "tp"),
        P("tp", "seq"),
        P(None, "grp", "seq", "tp"),
        P("grp"),
    )
    out_specs = (P("grp", "seq"), P("grp", None, "tp"))

    def body(*args):
        return on_device(mesh.shape["seq"], mesh.shape["tp"], *args)

    return jax.shard_map(
        body, mesh=mesh, in_specs=in_specs, out_specs=out_specs, check_vma=False
    )
```

time: 107 us -> 37.8 us (0.35)
  blocking collectives: 94.9 us -> 0 us
  waiting for transfers between devices: 0 us -> 14.7 us
  starting transfers between devices: 0 us -> 12.7 us
  matrix products: 6.52 us -> 0.24 us
  Pallas kernels: 0 us -> 3.27 us
  local copies, waits for them, and re-layouts: 2.77 us -> 4.43 us
    psum x3 -> x0, blocking collectives: 77.8 us -> none  [the longest x2 74.5 us: on_device(): lax.psum((query_part, keyval_part, squares), 'seq')]
    pmax x1 -> x0, blocking collectives: 17.1 us -> none  [on_device(): best_score = lax.pmax(block_max, 'seq')]
    ppermute x0 -> x9, waiting for transfers between devices: none -> 14.7 us  [partners(): lax.ppermute(value, axis, [(i, i ^ offset) for i in range(size)])]
    ppermute x0 -> x9, starting transfers between devices: none -> 12.7 us  [partners(): lax.ppermute(value, axis, [(i, i ^ offset) for i in range(size)])]
    dot_general x5 -> x0, matrix products: 6.15 us -> none  [the longest x1 2.84 us: on_device(): query_part = jnp.dot(scaled, query_proj, preferred_element_type=jnp.float32)]
    pallas_call x0 -> x4, Pallas kernels: none -> 3.27 us  [call(): pl.pallas_call(kernel, out_shape=outs, in_specs=[SMEM if a.dtype == jnp.i...]
    unnamed x10 -> x19, local copies, waits for them, and re-layouts: 2.11 us -> 3.82 us
  transfers between devices with their start and end apart: 0 -> 9, of which waited for: 0 -> 5; matrix products, arithmetic and copies ran while one was open for 0% -> 5% of each run, Pallas kernels for 0% -> 0%
where the time goes in v1:
time: 37.8 us; the launch traced here: 37.5 us
  waiting for transfers between devices  14.7 us (39%)
  starting transfers between devices  12.7 us (34%)
  local copies, waits for them, and re-layouts  4.43 us (12%)
  Pallas kernels  3.27 us (9%)
  other arithmetic  1.46 us (4%)
  between operations  0.73 us (2%)
    ppermute x9, waiting for transfers between devices, partners(): lax.ppermute(value, axis, [(i, i ^ offset) for i in range(size)])  14.7 us
    ppermute x9, starting transfers between devices, partners(): lax.ppermute(value, axis, [(i, i ^ offset) for i in range(size)])  12.7 us
    unnamed x19, local copies, waits for them, and re-layouts  3.82 us
    pallas_call x4, Pallas kernels, call(): pl.pallas_call(kernel, out_shape=outs, in_specs=[SMEM if a.dtype == jnp.i...  3.27 us
    add x1, other arithmetic, on_device(): first = first + other  0.83 us
  transfers between devices with their start and end apart: 9, of which 5 were waited for; matrix products, arithmetic and copies ran while one was open for 5% of the time, Pallas kernels for 0%

profile of v1, /device:TPU:0, one launch (start us, length us, event | category | flops | bytes accessed | tf_op | source)
XLA Modules:
  0.0 37.5 jit_solution(15579831697746804370)
XLA Ops:
  0.6 0.0 copy-start
  0.6 2.2 %copy-done = bf16[1024,2048]{1,0:T(8,128)(2,1)S(1)} copy-done((bf16[1024,2048]{1,0:T(8,128)(2,1)S(1)}, bf16[1024,2048]{1,0:T(8,128)(2,1)}, u32[]{:S(2)}) %copy-start) | copy-done | bytes 4194328
  2.8 0.0 copy-start.2
  2.8 0.7 %copy-done.2 = bf16[4,1024]{1,0:T(4,128)(2,1)S(1)} copy-done((bf16[4,1024]{1,0:T(4,128)(2,1)S(1)}, bf16[4,1024]{1,0:T(4,128)(2,1)}, u32[]{:S(2)}) %copy-start.2) | copy-done | bytes 8216
  3.5 0.0 copy-start.4
  3.5 0.7 %copy-done.4 = f32[1024]{0:T(1024)S(1)} copy-done((f32[1024]{0:T(1024)S(1)}, f32[1024]{0:T(1024)}, u32[]{:S(2)}) %copy-start.4) | copy-done | bytes 4120
  4.2 0.0 copy-start.7
  4.2 1.3 %shard_map.86 = f32[4,2176]{1,0:T(4,128)} custom-call(bf16[4,1024]{1,0:T(4,128)(2,1)S(1)} %copy-done.2, f32[1,1024]{1,0:T(1,128)S(1)} %bitcast.4, bf16[1024,2048]{1,0:T(8,128)(2,1)S(1)} %copy-done), custom_call_target="tpu_custom_call" | custom-call | flops 16777216 | bytes 16777216 | tf_op jit(solution)/shard_map/pallas_call | solution.py:25
  5.5 4.1 %collective-permute-start = (f32[4,2176]{1,0:T(4,128)}, f32[4,2176]{1,0:T(4,128)}, u32[]{:S(2)}, u32[]{:S(2)}) collective-permute-start(f32[4,2176]{1,0:T(4,128)} %shard_map.86), channel_id=1, source_target_pairs={{0,8},{2,10},{4,12},{6,14},{8,0},{10,2},{12,4},{14,6},{1,9},{3,11}... | collective-permute-start | bytes 104456 | tf_op jit(solution)/shard_map/ppermute | solution.py:54
  9.5 1.3 %collective-permute-start.1 = (f32[4,2176]{1,0:T(4,128)}, f32[4,2176]{1,0:T(4,128)}, u32[]{:S(2)}, u32[]{:S(2)}) collective-permute-start(f32[4,2176]{1,0:T(4,128)} %shard_map.86), channel_id=1, source_target_pairs={{0,12},{2,14},{4,8},{6,10},{8,4},{10,6},{12,0},{14,2},{1,13},{3,15... | collective-permute-start | bytes 104456 | tf_op jit(solution)/shard_map/ppermute | solution.py:54
  10.9 0.2 collective-permute-start.2
  11.1 0.0 copy-done.7
  11.1 0.0 copy-start.8
  11.1 0.0 copy-start.3
  11.1 0.0 copy-start.5
  11.1 0.0 copy-start.6
  11.2 0.0 copy-start.1
  11.2 1.6 %collective-permute-start.4 = (f32[2,4,64,256]{3,2,1,0:T(8,128)S(1)}, f32[2,4,64,256]{3,2,1,0:T(8,128)S(1)}, u32[]{:S(2)}, u32[]{:S(2)}) collective-permute-start(f32[2,4,64,256]{3,2,1,0:T(8,128)S(1)} %shard_map.87.near_ref), channel_id=1, source_target_pairs={{0,2},{2,0},{4,6},{6,4},{8,10},{10,8},{12,14},{14,12},{1,3},{3,1},... | collective-permute-start | bytes 1572872 | tf_op jit(solution)/shard_map/ppermute | solution.py:54
  12.8 0.0 copy-done.8
  12.8 0.2 copy.9
  13.0 0.0 copy-done.3
  13.0 0.0 copy-done.5
  13.0 0.2 fusion.2
  13.3 0.0 collective-permute-done
  13.3 2.3 %collective-permute-done.1 = f32[4,2176]{1,0:T(4,128)} collective-permute-done((f32[4,2176]{1,0:T(4,128)}, f32[4,2176]{1,0:T(4,128)}, u32[]{:S(2)}, u32[]{:S(2)}) %collective-permute-start.1) | collective-permute-done | bytes 34848 | tf_op jit(solution)/shard_map/ppermute | solution.py:54
  15.6 0.0 collective-permute-done.2
  15.6 0.8 %add_add_fusion = f32[4,2176]{1,0:T(4,128)S(1)} fusion(f32[4,2176]{1,0:T(4,128)} %collective-permute-done.2, f32[4,2176]{1,0:T(4,128)} %collective-permute-done.1, f32[4,2176]{1,0:T(4,128)} %shard_map.86, f32[4,2176]{1,0:T(4,128)} %collective-permute-done), kind=kLoop, calls=%fused_computation.1 | loop fusion | flops 26112 | bytes 174080 | tf_op jit(solution)/shard_map/add | solution.py:255
  16.5 1.6 %collective-permute-start.3 = (f32[4,2688]{1,0:T(4,128)S(1)}, f32[4,2688]{1,0:T(4,128)S(1)}, u32[]{:S(2)}, u32[]{:S(2)}) collective-permute-start(f32[4,2688]{1,0:T(4,128)S(1)} %pad_maximum_fusion.mine_ref), channel_id=1, source_target_pairs={{0,2},{2,0},{4,6},{6,4},{8,10},{10,8},{12,14},{14,12},{1,3},{3,1},... | collective-permute-start | bytes 129032 | tf_op jit(solution)/shard_map/ppermute | solution.py:54
  18.0 7.3 %collective-permute-done.3.other_ref = f32[4,2688]{1,0:T(4,128)S(1)} collective-permute-done((f32[4,2688]{1,0:T(4,128)S(1)}, f32[4,2688]{1,0:T(4,128)S(1)}, u32[]{:S(2)}, u32[]{:S(2)}) %collective-permute-start.3) | collective-permute-done | bytes 43040 | tf_op jit(solution)/shard_map/ppermute | solution.py:54
  25.3 0.0 collective-permute-done.4.far_ref
  25.3 0.0 copy-done.6
  25.3 1.0 %shard_map.88 = (f32[88,128]{1,0:T(8,128)S(1)}, bf16[64,128]{1,0:T(8,128)(2,1)S(1)}, f32[4,128]{1,0:T(4,128)S(1)}) custom-call(s32[4]{0:T(128)S(1)} %copy-done.6, f32[4,2688]{1,0:T(4,128)S(1)} %pad_maximum_fusion.mine_ref, f32[4,2688]{1,0:T(4,128)S(1)} %collective-permute-done.3.other_ref, f32[2,4,64,256]{3,2,1,0:T(8,128)S(1)} %shard_map.87.near_ref, ...), custom_call_target="tpu_custom_call" | custom-call | flops 8388608 | bytes 16777216 | tf_op jit(solution)/shard_map/pallas_call | solution.py:25
  26.3 2.6 %collective-permute-start.5 = (f32[88,128]{1,0:T(8,128)S(1)}, f32[88,128]{1,0:T(8,128)S(1)}, u32[]{:S(2)}, u32[]{:S(2)}) collective-permute-start(f32[88,128]{1,0:T(8,128)S(1)} %get-tuple-element.9.refs_0_), channel_id=1, source_target_pairs={{0,8},{2,10},{4,12},{6,14},{8,0},{10,2},{12,4},{14,6},{1,9},{3,11}... | collective-permute-start | bytes 135176 | tf_op jit(solution)/shard_map/ppermute | solution.py:54
  28.9 1.3 %collective-permute-start.6 = (f32[88,128]{1,0:T(8,128)S(1)}, f32[88,128]{1,0:T(8,128)S(1)}, u32[]{:S(2)}, u32[]{:S(2)}) collective-permute-start(f32[88,128]{1,0:T(8,128)S(1)} %get-tuple-element.9.refs_0_), channel_id=1, source_target_pairs={{0,12},{2,14},{4,8},{6,10},{8,4},{10,6},{12,0},{14,2},{1,13},{3,15... | collective-permute-start | bytes 135176 | tf_op jit(solution)/shard_map/ppermute | solution.py:54
  30.2 0.0 collective-permute-start.7
  30.2 1.6 %collective-permute-done.5.refs_1_ = f32[88,128]{1,0:T(8,128)S(1)} collective-permute-done((f32[88,128]{1,0:T(8,128)S(1)}, f32[88,128]{1,0:T(8,128)S(1)}, u32[]{:S(2)}, u32[]{:S(2)}) %collective-permute-start.5) | collective-permute-done | bytes 45088 | tf_op jit(solution)/shard_map/ppermute | solution.py:54
  31.8 2.9 %collective-permute-done.6.refs_2_ = f32[88,128]{1,0:T(8,128)S(1)} collective-permute-done((f32[88,128]{1,0:T(8,128)S(1)}, f32[88,128]{1,0:T(8,128)S(1)}, u32[]{:S(2)}, u32[]{:S(2)}) %collective-permute-start.6) | collective-permute-done | bytes 45088 | tf_op jit(solution)/shard_map/ppermute | solution.py:54
  34.7 0.0 collective-permute-done.7.refs_3_
  34.7 0.0 copy-done.1
  34.7 1.0 %shard_map.89 = (f32[4,1024]{1,0:T(4,128)S(1)}, f32[4,512]{1,0:T(4,128)S(1)}) custom-call(bf16[64,128]{1,0:T(8,128)(2,1)S(1)} %get-tuple-element.7.query_ref, f32[4,128]{1,0:T(4,128)S(1)} %get-tuple-element.8.scale_ref, bf16[2048,1024]{1,0:T(8,128)(2,1)S(1)} %copy-done.1, f32[88,128]{1,0:T(8,128)S(1)} %get-tuple-element.9.refs_0_, ...), custom_call_target="tpu_custom_call" | custom-call | flops 16777216 | bytes 16777216 | tf_op jit(solution)/shard_map/pallas_call | solution.py:25
  35.7 0.0 collective-permute-start.8
  35.8 0.6 %reshape.16 = bf16[4,2,256]{2,1,0:T(2,128)(2,1)} reshape(bf16[4,512]{1,0:T(4,128)(2,1)S(1)} %convert_element_type.15) | data formatting | bytes 8192 | tf_op jit(solution)/shard_map/reshape | solution.py:293
  36.4 0.6 %collective-permute-done.8 = f32[4,1024]{1,0:T(4,128)S(1)} collective-permute-done((f32[4,1024]{1,0:T(4,128)S(1)}, f32[4,1024]{1,0:T(4,128)S(1)}, u32[]{:S(2)}, u32[]{:S(2)}) %collective-permute-start.8) | collective-permute-done | bytes 16416 | tf_op jit(solution)/shard_map/ppermute | solution.py:54
  36.9 0.6 %fusion.1 = bf16[4,1024]{1,0:T(4,128)(2,1)} fusion(bf16[4,1024]{1,0:T(4,128)(2,1)S(1)} %copy-done.3, f32[4,1024]{1,0:T(4,128)S(1)} %get-tuple-element.10, f32[4,1024]{1,0:T(4,128)S(1)} %collective-permute-done.8), kind=kLoop, calls=%fused_computation.5 | loop fusion | flops 16384 | bytes 49152 | tf_op jit(solution)/shard_map/convert_element_type | solution.py:292
  (3 shorter events, 0.1 us)
Async XLA Ops:
  0.6 2.2 %copy-start = (bf16[1024,2048]{1,0:T(8,128)(2,1)S(1)}, bf16[1024,2048]{1,0:T(8,128)(2,1)}, u32[]{:S(2)}) copy-start(bf16[1024,2048]{1,0:T(8,128)(2,1)} %proj_ref.2) | copy-start | bytes 12582916
  2.8 0.7 %copy-start.2 = (bf16[4,1024]{1,0:T(4,128)(2,1)S(1)}, bf16[4,1024]{1,0:T(4,128)(2,1)}, u32[]{:S(2)}) copy-start(bf16[4,1024]{1,0:T(4,128)(2,1)} %hidden_ref.1) | copy-start | bytes 24580
  3.5 0.7 %copy-start.4 = (f32[1024]{0:T(1024)S(1)}, f32[1024]{0:T(1024)}, u32[]{:S(2)}) copy-start(f32[1024]{0:T(1024)} %param.8) | copy-start | bytes 12292
  4.2 6.9 %copy-start.7 = (bf16[2,4,64,256]{3,2,1,0:T(8,128)(2,1)S(1)}, bf16[2,4,64,256]{3,2,1,0:T(8,128)(2,1)}, u32[]{:S(2)}) copy-start(bf16[2,4,64,256]{3,2,1,0:T(8,128)(2,1)} %cache_ref.1) | copy-start | bytes 786436
  5.5 7.8 %collective-permute-start = (f32[4,2176]{1,0:T(4,128)}, f32[4,2176]{1,0:T(4,128)}, u32[]{:S(2)}, u32[]{:S(2)}) collective-permute-start(f32[4,2176]{1,0:T(4,128)} %shard_map.86), channel_id=1, source_target_pairs={{0,8},{2,10},{4,12},{6,14},{8,0},{10,2},{12,4},{14,6},{1,9},{3,11}... | collective-permute-start | bytes 104456 | tf_op jit(solution)/shard_map/ppermute | solution.py:54
  9.5 6.0 %collective-permute-start.1 = (f32[4,2176]{1,0:T(4,128)}, f32[4,2176]{1,0:T(4,128)}, u32[]{:S(2)}, u32[]{:S(2)}) collective-permute-start(f32[4,2176]{1,0:T(4,128)} %shard_map.86), channel_id=1, source_target_pairs={{0,12},{2,14},{4,8},{6,10},{8,4},{10,6},{12,0},{14,2},{1,13},{3,15... | collective-permute-start | bytes 104456 | tf_op jit(solution)/shard_map/ppermute | solution.py:54
  10.9 4.7 %collective-permute-start.2 = (f32[4,2176]{1,0:T(4,128)}, f32[4,2176]{1,0:T(4,128)}, u32[]{:S(2)}, u32[]{:S(2)}) collective-permute-start(f32[4,2176]{1,0:T(4,128)} %shard_map.86), channel_id=1, source_target_pairs={{0,4},{2,6},{4,0},{6,2},{8,12},{10,14},{12,8},{14,10},{1,5},{3,7},... | collective-permute-start | bytes 104456 | tf_op jit(solution)/shard_map/ppermute | solution.py:54
  11.1 1.6 %copy-start.8 = (bf16[1024,2,256]{2,1,0:T(2,128)(2,1)S(1)}, bf16[1024,2,256]{2,1,0:T(2,128)(2,1)}, u32[]{:S(2)}) copy-start(bf16[1024,2,256]{2,1,0:T(2,128)(2,1)} %param.10) | copy-start | bytes 3145732
  11.1 1.9 %copy-start.3 = (bf16[4,1024]{1,0:T(4,128)(2,1)S(1)}, bf16[4,1024]{1,0:T(4,128)(2,1)}, u32[]{:S(2)}) copy-start(bf16[4,1024]{1,0:T(4,128)(2,1)} %hidden_ref.1) | copy-start | bytes 24580
  11.1 1.9 %copy-start.5 = (f32[1024]{0:T(1024)S(1)}, f32[1024]{0:T(1024)}, u32[]{:S(2)}) copy-start(f32[1024]{0:T(1024)} %param.8) | copy-start | bytes 12292
  11.1 14.2 %copy-start.6 = (s32[4]{0:T(128)S(1)}, s32[4]{0:T(128)}, u32[]{:S(2)}) copy-start(s32[4]{0:T(128)} %lengths_ref.1) | copy-start | bytes 52
  11.2 23.6 %copy-start.1 = (bf16[2048,1024]{1,0:T(8,128)(2,1)S(1)}, bf16[2048,1024]{1,0:T(8,128)(2,1)}, u32[]{:S(2)}) copy-start(bf16[2048,1024]{1,0:T(8,128)(2,1)} %proj_ref.3) | copy-start | bytes 12582916
  11.2 14.1 %collective-permute-start.4 = (f32[2,4,64,256]{3,2,1,0:T(8,128)S(1)}, f32[2,4,64,256]{3,2,1,0:T(8,128)S(1)}, u32[]{:S(2)}, u32[]{:S(2)}) collective-permute-start(f32[2,4,64,256]{3,2,1,0:T(8,128)S(1)} %shard_map.87.near_ref), channel_id=1, source_target_pairs={{0,2},{2,0},{4,6},{6,4},{8,10},{10,8},{12,14},{14,12},{1,3},{3,1},... | collective-permute-start | bytes 1572872 | tf_op jit(solution)/shard_map/ppermute | solution.py:54
  16.5 8.8 %collective-permute-start.3 = (f32[4,2688]{1,0:T(4,128)S(1)}, f32[4,2688]{1,0:T(4,128)S(1)}, u32[]{:S(2)}, u32[]{:S(2)}) collective-permute-start(f32[4,2688]{1,0:T(4,128)S(1)} %pad_maximum_fusion.mine_ref), channel_id=1, source_target_pairs={{0,2},{2,0},{4,6},{6,4},{8,10},{10,8},{12,14},{14,12},{1,3},{3,1},... | collective-permute-start | bytes 129032 | tf_op jit(solution)/shard_map/ppermute | solution.py:54
  26.3 5.6 %collective-permute-start.5 = (f32[88,128]{1,0:T(8,128)S(1)}, f32[88,128]{1,0:T(8,128)S(1)}, u32[]{:S(2)}, u32[]{:S(2)}) collective-permute-start(f32[88,128]{1,0:T(8,128)S(1)} %get-tuple-element.9.refs_0_), channel_id=1, source_target_pairs={{0,8},{2,10},{4,12},{6,14},{8,0},{10,2},{12,4},{14,6},{1,9},{3,11}... | collective-permute-start | bytes 135176 | tf_op jit(solution)/shard_map/ppermute | solution.py:54
  28.9 5.9 %collective-permute-start.6 = (f32[88,128]{1,0:T(8,128)S(1)}, f32[88,128]{1,0:T(8,128)S(1)}, u32[]{:S(2)}, u32[]{:S(2)}) collective-permute-start(f32[88,128]{1,0:T(8,128)S(1)} %get-tuple-element.9.refs_0_), channel_id=1, source_target_pairs={{0,12},{2,14},{4,8},{6,10},{8,4},{10,6},{12,0},{14,2},{1,13},{3,15... | collective-permute-start | bytes 135176 | tf_op jit(solution)/shard_map/ppermute | solution.py:54
  30.2 4.5 %collective-permute-start.7 = (f32[88,128]{1,0:T(8,128)S(1)}, f32[88,128]{1,0:T(8,128)S(1)}, u32[]{:S(2)}, u32[]{:S(2)}) collective-permute-start(f32[88,128]{1,0:T(8,128)S(1)} %get-tuple-element.9.refs_0_), channel_id=1, source_target_pairs={{0,4},{2,6},{4,0},{6,2},{8,12},{10,14},{12,8},{14,10},{1,5},{3,7},... | collective-permute-start | bytes 135176 | tf_op jit(solution)/shard_map/ppermute | solution.py:54
  35.7 1.2 %collective-permute-start.8 = (f32[4,1024]{1,0:T(4,128)S(1)}, f32[4,1024]{1,0:T(4,128)S(1)}, u32[]{:S(2)}, u32[]{:S(2)}) collective-permute-start(f32[4,1024]{1,0:T(4,128)S(1)} %get-tuple-element.10), channel_id=1, source_target_pairs={{0,1},{1,0},{2,3},{3,2},{4,5},{5,4},{6,7},{7,6},{8,9},{9,8},{10,11... | collective-permute-start | bytes 49160 | tf_op jit(solution)/shard_map/ppermute | solution.py:54

commit v2 on v1

--- a/solution.py
+++ b/solution.py
@@ -15,7 +15,12 @@
 
 
 COVER = 16 << 20
-COVER_OPS = 1 << 30
+COVER_OPS = 1 << 22
+
+ORDERS = (
+    lambda low, high: (high, low | high, low),
+    lambda low, high: (low | high, high, low),
+)
 
 VMEM = pl.BlockSpec(memory_space=pltpu.VMEM)
 SMEM = pl.BlockSpec(memory_space=pltpu.SMEM)
@@ -34,24 +39,26 @@
     )(*ins)
 
 
-def stages(size):
-    bits = size.bit_length() - 1
+def pair_bit(seq, core):
+    return core % min(2, seq.bit_length() - 1)
+
+
+def stages(seq, core):
+    bits = [1 << b for b in range(seq.bit_length() - 1) if b != pair_bit(seq, core)]
     out = []
-    bit = 1
-    while bit < bits:
-        if bit + 1 < bits:
-            out.append((2 << bit, 3 << bit, 1 << bit))
-            bit += 2
-        else:
-            out.append((1 << bit,))
-            bit += 1
-    return out
-
-
-def partners(value, axis, size, offsets):
+    while len(bits) > 1:
+        low, high, *bits = bits
+        out.append(ORDERS[core % 2](low, high))
+    return out + [(bit,) for bit in bits]
+
+
+def exchange(value, seq, tp, offsets):
     got = []
-    for offset in offsets:
-        got.append(lax.ppermute(value, axis, [(i, i ^ offset) for i in range(size)]))
+    for pair in zip(*offsets):
+        moves = [
+            (i * tp + core, (i ^ pair[core]) * tp + core) for i in range(seq) for core in range(tp)
+        ]
+        got.append(lax.ppermute(value, ("seq", "tp"), moves))
     return got
 
 
@@ -68,14 +75,36 @@
     out_ref[:, :width] = jnp.dot(scaled, proj_ref[...], preferred_element_type=jnp.float32)
 
 
+def blocks_kernel(pair_offset, lengths_ref, near_ref, far_ref, keys_ref, values_ref, live_ref):
+    rows, ctx = near_ref.shape[1:3]
+    shape = live_ref.shape
+    request = lax.broadcasted_iota(jnp.int32, shape, 0) % rows
+    lane = lax.broadcasted_iota(jnp.int32, shape, 1)
+    length = jnp.zeros(shape, jnp.int32)
+    for r in range(rows):
+        length = jnp.where(request == r, lengths_ref[r], length)
+    rank = lax.axis_index("seq")
+    pair = rank ^ pair_offset()
+    position = jnp.where(lane < ctx, rank * ctx + lane, pair * ctx + lane - ctx)
+    live_ref[...] = jnp.where(position < length, 1.0, 0.0)
+    for kind, out_ref in enumerate((keys_ref, values_ref)):
+        for k in range(out_ref.shape[0]):
+            for r in range(rows):
+                for side, ref in enumerate((near_ref, far_ref)):
+                    at = (2 * r + side) * ctx
+                    out_ref[k, at : at + ctx, :] = ref[
+                        kind, r, :, k * HEAD_DIM : (k + 1) * HEAD_DIM
+                    ].astype(jnp.bfloat16)
+
+
 def attend_kernel(
-    features, width, lengths_ref, mine_ref, other_ref, near_ref, far_ref,
+    features, width, mine_ref, other_ref, keys_ref, values_ref, live_ref,
     packed_ref, query_ref, scale_ref,
 ):
     rows = mine_ref.shape[0]
     heads = width // HEAD_DIM
-    ctx = near_ref.shape[2]
-    kv_heads = near_ref.shape[3] // HEAD_DIM
+    kv_heads = keys_ref.shape[0]
+    ctx = keys_ref.shape[1] // rows // 2
     share = heads // kv_heads * rows
     split = heads * rows
     scale = lax.rsqrt(
@@ -93,32 +122,13 @@
     ).astype(jnp.bfloat16)
     query_ref[...] = query
     request = lax.broadcasted_iota(jnp.int32, (split, 2 * ctx), 0) % rows
-    lane = lax.broadcasted_iota(jnp.int32, (split, 2 * ctx), 1)
-    near = lane < ctx
-    length = jnp.zeros((split, 2 * ctx), jnp.int32)
-    for r in range(rows):
-        length = jnp.where(request == r, lengths_ref[r], length)
-    rank = lax.axis_index("seq")
-    pair = rank + 1 - 2 * (rank % 2)
-    position = jnp.where(near, rank * ctx + lane, pair * ctx + lane - ctx)
-    live = position < length
-
-    def blocks(kind, k):
-        cut = slice(k * HEAD_DIM, (k + 1) * HEAD_DIM)
-        return jnp.concatenate(
-            [
-                ref[kind, r, :, cut].astype(jnp.bfloat16)
-                for r in range(rows)
-                for ref in (near_ref, far_ref)
-            ],
-            axis=0,
-        )
-
+    near = lax.broadcasted_iota(jnp.int32, (split, 2 * ctx), 1) < ctx
+    live = live_ref[...] > 0
     scores = []
     for k in range(kv_heads):
         all_scores = lax.dot_general(
             query[k * share : (k + 1) * share],
-            blocks(0, k),
+            keys_ref[k],
             (((1,), (1,)), ((), ())),
             preferred_element_type=jnp.float32,
         )
@@ -150,7 +160,7 @@
             ],
             axis=0,
         ).astype(jnp.bfloat16)
-        outs = jnp.dot(spread, blocks(1, k), preferred_element_type=jnp.float32)
+        outs = jnp.dot(spread, values_ref[k], preferred_element_type=jnp.float32)
         packed_ref[cut, :] = factors[0][cut] * outs[:share] + factors[1][cut] * outs[share:]
     column = lax.broadcasted_iota(jnp.int32, (split, HEAD_DIM), 1)
     pair = jnp.where(column == 0, top, jnp.where(column == 1, total, 0.0))
@@ -232,6 +242,12 @@
     width = query_proj.shape[1]
     split = rows * width // HEAD_DIM
     one_float = hidden.astype(f32)
+    pairs = [(1 << pair_bit(seq, core),) for core in range(tp)]
+    rounds = list(zip(*(stages(seq, core) for core in range(tp))))
+
+    def pair_offset():
+        core = lax.axis_index("tp")
+        return sum(jnp.where(core == c, offset, 0) for c, (offset,) in enumerate(pairs))
 
     near = call(
         widen_kernel,
@@ -241,7 +257,7 @@
         COVER,
         COVER_OPS,
     )[0]
-    far = partners(near, "seq", seq, (1,))[0]
+    far = exchange(near, seq, tp, pairs)[0]
 
     first = call(
         query_kernel,
@@ -250,16 +266,26 @@
         2 * rows * feature_dev * width,
         COVER,
     )[0]
-    for offsets in stages(seq):
-        for other in partners(first, "seq", seq, offsets):
+    for offsets in rounds:
+        for other in exchange(first, seq, tp, offsets):
             first = first + other
     scaled = (one_float * norm_gain).astype(jnp.bfloat16)
     keyval_part = jnp.dot(
         scaled, keyval_proj.reshape(feature_dev, 2 * kv_width), preferred_element_type=f32
     )
     first = jnp.concatenate([first, keyval_part], axis=1)
-    second = partners(first, "seq", seq, (1,))[0]
-
+    second = exchange(first, seq, tp, pairs)[0]
+
+    block = jax.ShapeDtypeStruct(
+        (kv_width // HEAD_DIM, 2 * rows * keyval_cache.shape[2], HEAD_DIM), jnp.bfloat16
+    )
+    keys, values, live = call(
+        functools.partial(blocks_kernel, pair_offset),
+        [block, block, jax.ShapeDtypeStruct((split, 2 * keyval_cache.shape[2]), f32)],
+        [lengths, near, far],
+        0,
+        4 * near.size,
+    )
     pack = jax.ShapeDtypeStruct((split + 8 + rows * 2 * kv_width // HEAD_DIM, HEAD_DIM), f32)
     packed, query, scale = call(
         functools.partial(attend_kernel, float(seq * feature_dev), width),
@@ -268,14 +294,13 @@
             jax.ShapeDtypeStruct((split, HEAD_DIM), jnp.bfloat16),
             jax.ShapeDtypeStruct((rows, HEAD_DIM), f32),
         ],
-        [lengths, first, second, near, far],
+        [first, second, keys, values, live],
         16 * split * keyval_cache.shape[2] * HEAD_DIM,
         COVER,
     )
-    todo = stages(seq)
-    for place, offsets in enumerate(todo):
-        parts = [packed] + partners(packed, "seq", seq, offsets)
-        if place < len(todo) - 1:
+    for place, offsets in enumerate(rounds):
+        parts = [packed] + exchange(packed, seq, tp, offsets)
+        if place < len(rounds) - 1:
             packed = call(functools.partial(merge_kernel, split), [pack], parts, 0, COVER)[0]
     term, new_keyval = call(
         functools.partial(output_kernel, len(parts)),
@@ -288,7 +313,7 @@
         COVER,
     )
     for bit in range(tp.bit_length() - 1):
-        term = term + partners(term, "tp", tp, (1 << bit,))[0]
+        term = term + lax.ppermute(term, "tp", [(i, i ^ (1 << bit)) for i in range(tp)])
     hidden_out = (one_float + term).astype(jnp.bfloat16)
     return (hidden_out, new_keyval.astype(jnp.bfloat16).reshape(rows, 2, kv_width))
 

time: 37.8 us -> 33.3 us (0.88)
  waiting for transfers between devices: 14.7 us -> 11.5 us
  other arithmetic: 1.46 us -> 0.65 us
  Pallas kernels: 3.27 us -> 2.71 us
    ppermute x9, waiting for transfers between devices: 14.7 us -> 11.5 us  [the longest x8 10.9 us: exchange(): got.append(lax.ppermute(value, ('seq', 'tp'), moves))]
    add x1, other arithmetic: 0.83 us -> 0.02 us  [on_device(): first = first + other]
    pallas_call x4 -> x5, Pallas kernels: 3.27 us -> 2.71 us  [call(): pl.pallas_call(kernel, out_shape=outs, in_specs=[SMEM if a.dtype == jnp.i...]
  transfers between devices with their start and end apart: 9 -> 9, of which waited for: 5 -> 7; matrix products, arithmetic and copies ran while one was open for 5% -> 3% of each run, Pallas kernels for 0% -> 2%
where the time goes in v2:
time: 33.3 us; the launch traced here: 33 us
  starting transfers between devices  12.8 us (38%)
  waiting for transfers between devices  11.5 us (35%)
  local copies, waits for them, and re-layouts  4.44 us (13%)
  Pallas kernels  2.71 us (8%)
  between operations  0.73 us (2%)
  other arithmetic  0.65 us (2%)
    ppermute x8, starting transfers between devices, exchange(): got.append(lax.ppermute(value, ('seq', 'tp'), moves))  12.8 us
    ppermute x8, waiting for transfers between devices, exchange(): got.append(lax.ppermute(value, ('seq', 'tp'), moves))  10.9 us
    unnamed x19, local copies, waits for them, and re-layouts  3.83 us
    pallas_call x5, Pallas kernels, call(): pl.pallas_call(kernel, out_shape=outs, in_specs=[SMEM if a.dtype == jnp.i...  2.71 us
  transfers between devices with their start and end apart: 9, of which 7 were waited for; matrix products, arithmetic and copies ran while one was open for 3% of the time, Pallas kernels for 2%

profile of v2, /device:TPU:0, one launch (start us, length us, event | category | flops | bytes accessed | tf_op | source)
XLA Modules:
  0.0 33.0 jit_solution(9620034528361700612)
XLA Ops:
  0.6 0.0 copy-start
  0.6 2.2 %copy-done = bf16[1024,2048]{1,0:T(8,128)(2,1)S(1)} copy-done((bf16[1024,2048]{1,0:T(8,128)(2,1)S(1)}, bf16[1024,2048]{1,0:T(8,128)(2,1)}, u32[]{:S(2)}) %copy-start) | copy-done | bytes 4194328
  2.8 0.0 copy-start.2
  2.8 0.7 %copy-done.2 = bf16[4,1024]{1,0:T(4,128)(2,1)S(1)} copy-done((bf16[4,1024]{1,0:T(4,128)(2,1)S(1)}, bf16[4,1024]{1,0:T(4,128)(2,1)}, u32[]{:S(2)}) %copy-start.2) | copy-done | bytes 8216
  3.5 0.0 copy-start.4
  3.5 0.7 %copy-done.4 = f32[1024]{0:T(1024)S(1)} copy-done((f32[1024]{0:T(1024)S(1)}, f32[1024]{0:T(1024)}, u32[]{:S(2)}) %copy-start.4) | copy-done | bytes 4120
  4.2 0.0 copy-start.7
  4.2 0.6 %shard_map.86 = f32[4,2176]{1,0:T(4,128)S(1)} custom-call(bf16[4,1024]{1,0:T(4,128)(2,1)S(1)} %copy-done.2, f32[1,1024]{1,0:T(1,128)S(1)} %bitcast.4, bf16[1024,2048]{1,0:T(8,128)(2,1)S(1)} %copy-done), custom_call_target="tpu_custom_call" | custom-call | flops 16777216 | bytes 16777216 | tf_op jit(solution)/shard_map/pallas_call | solution.py:30
  4.9 0.0 copy-start.8
  4.9 0.0 copy-start.3
  4.9 0.0 copy-start.5
  4.9 0.0 copy-start.6
  4.9 3.1 %collective-permute-start.2 = (f32[4,2176]{1,0:T(4,128)S(1)}, f32[4,2176]{1,0:T(4,128)S(1)}, u32[]{:S(2)}, u32[]{:S(2)}) collective-permute-start(f32[4,2176]{1,0:T(4,128)S(1)} %shard_map.86), channel_id=1, source_target_pairs={{0,4},{1,3},{2,6},{3,1},{4,0},{5,7},{6,2},{7,5},{8,12},{9,11},{10,... | collective-permute-start | bytes 104456 | tf_op jit(solution)/shard_map/ppermute | solution.py:61
  8.0 2.5 %collective-permute-start.1 = (f32[4,2176]{1,0:T(4,128)S(1)}, f32[4,2176]{1,0:T(4,128)S(1)}, u32[]{:S(2)}, u32[]{:S(2)}) collective-permute-start(f32[4,2176]{1,0:T(4,128)S(1)} %shard_map.86), channel_id=1, source_target_pairs={{0,12},{1,9},{2,14},{3,11},{4,8},{5,13},{6,10},{7,15},{8,4},{9,1},... | collective-permute-start | bytes 104456 | tf_op jit(solution)/shard_map/ppermute | solution.py:61
  10.5 0.1 collective-permute-start
  10.6 0.0 copy-done.7
  10.6 0.0 copy-start.1
  10.6 1.6 %collective-permute-start.4 = (f32[2,4,64,256]{3,2,1,0:T(8,128)S(1)}, f32[2,4,64,256]{3,2,1,0:T(8,128)S(1)}, u32[]{:S(2)}, u32[]{:S(2)}) collective-permute-start(f32[2,4,64,256]{3,2,1,0:T(8,128)S(1)} %shard_map.87.near_ref), channel_id=1, source_target_pairs={{0,2},{1,5},{2,0},{3,7},{4,6},{5,1},{6,4},{7,3},{8,10},{9,13},{10,... | collective-permute-start | bytes 1572872 | tf_op jit(solution)/shard_map/ppermute | solution.py:61
  12.2 0.0 copy-done.8
  12.2 0.2 copy.9
  12.4 0.0 copy-done.3
  12.5 0.0 copy-done.5
  12.5 0.2 fusion.2
  12.7 0.0 collective-permute-done.2
  12.7 1.2 %collective-permute-done.1 = f32[4,2176]{1,0:T(4,128)S(1)} collective-permute-done((f32[4,2176]{1,0:T(4,128)S(1)}, f32[4,2176]{1,0:T(4,128)S(1)}, u32[]{:S(2)}, u32[]{:S(2)}) %collective-permute-start.1) | collective-permute-done | bytes 34848 | tf_op jit(solution)/shard_map/ppermute | solution.py:61
  13.9 1.6 %collective-permute-done = f32[4,2176]{1,0:T(4,128)S(1)} collective-permute-done((f32[4,2176]{1,0:T(4,128)S(1)}, f32[4,2176]{1,0:T(4,128)S(1)}, u32[]{:S(2)}, u32[]{:S(2)}) %collective-permute-start) | collective-permute-done | bytes 34848 | tf_op jit(solution)/shard_map/ppermute | solution.py:61
  15.6 1.6 %collective-permute-start.3 = (f32[4,2688]{1,0:T(4,128)S(1)}, f32[4,2688]{1,0:T(4,128)S(1)}, u32[]{:S(2)}, u32[]{:S(2)}) collective-permute-start(f32[4,2688]{1,0:T(4,128)S(1)} %pad_maximum_fusion.mine_ref), channel_id=1, source_target_pairs={{0,2},{1,5},{2,0},{3,7},{4,6},{5,1},{6,4},{7,3},{8,10},{9,13},{10,... | collective-permute-start | bytes 129032 | tf_op jit(solution)/shard_map/ppermute | solution.py:61
  17.2 3.1 %collective-permute-done.4.far_ref = f32[2,4,64,256]{3,2,1,0:T(8,128)S(1)} collective-permute-done((f32[2,4,64,256]{3,2,1,0:T(8,128)S(1)}, f32[2,4,64,256]{3,2,1,0:T(8,128)S(1)}, u32[]{:S(2)}, u32[]{:S(2)}) %collective-permute-start.4) | collective-permute-done | bytes 524320 | tf_op jit(solution)/shard_map/ppermute | solution.py:61
  20.3 0.0 copy-done.6
  20.3 0.6 %shard_map.88 = (bf16[2,512,128]{2,1,0:T(8,128)(2,1)S(1)}, bf16[2,512,128]{2,1,0:T(8,128)(2,1)S(1)}, f32[64,128]{1,0:T(8,128)S(1)}) custom-call(s32[4]{0:T(128)S(1)} %copy-done.6, f32[2,4,64,256]{3,2,1,0:T(8,128)S(1)} %shard_map.87.near_ref, f32[2,4,64,256]{3,2,1,0:T(8,128)S(1)} %collective-permute-done.4.far_ref), custom_call_target="tpu_custom_call" | custom-call | bytes 524288 | tf_op jit(solution)/shard_map/pallas_call | solution.py:30
  20.9 0.0 collective-permute-done.3.other_ref
  20.9 0.4 %shard_map.89 = (f32[88,128]{1,0:T(8,128)S(1)}, bf16[64,128]{1,0:T(8,128)(2,1)S(1)}, f32[4,128]{1,0:T(4,128)S(1)}) custom-call(f32[4,2688]{1,0:T(4,128)S(1)} %pad_maximum_fusion.mine_ref, f32[4,2688]{1,0:T(4,128)S(1)} %collective-permute-done.3.other_ref, bf16[2,512,128]{2,1,0:T(8,128)(2,1)S(1)} %get-tuple-element.10.keys_ref, ...), custom_call_target="tpu_custom_call" | custom-call | flops 8388608 | bytes 16777216 | tf_op jit(solution)/shard_map/pallas_call | solution.py:30
  21.3 1.5 %collective-permute-start.7 = (f32[88,128]{1,0:T(8,128)S(1)}, f32[88,128]{1,0:T(8,128)S(1)}, u32[]{:S(2)}, u32[]{:S(2)}) collective-permute-start(f32[88,128]{1,0:T(8,128)S(1)} %get-tuple-element.15.refs_0_), channel_id=1, source_target_pairs={{0,4},{1,3},{2,6},{3,1},{4,0},{5,7},{6,2},{7,5},{8,12},{9,11},{10,... | collective-permute-start | bytes 135176 | tf_op jit(solution)/shard_map/ppermute | solution.py:61
  22.9 2.4 %collective-permute-start.6 = (f32[88,128]{1,0:T(8,128)S(1)}, f32[88,128]{1,0:T(8,128)S(1)}, u32[]{:S(2)}, u32[]{:S(2)}) collective-permute-start(f32[88,128]{1,0:T(8,128)S(1)} %get-tuple-element.15.refs_0_), channel_id=1, source_target_pairs={{0,12},{1,9},{2,14},{3,11},{4,8},{5,13},{6,10},{7,15},{8,4},{9,1},... | collective-permute-start | bytes 135176 | tf_op jit(solution)/shard_map/ppermute | solution.py:61
  25.3 0.0 collective-permute-start.5
  25.3 0.6 %collective-permute-done.7.refs_3_ = f32[88,128]{1,0:T(8,128)S(1)} collective-permute-done((f32[88,128]{1,0:T(8,128)S(1)}, f32[88,128]{1,0:T(8,128)S(1)}, u32[]{:S(2)}, u32[]{:S(2)}) %collective-permute-start.7) | collective-permute-done | bytes 45088 | tf_op jit(solution)/shard_map/ppermute | solution.py:61
  25.9 3.2 %collective-permute-done.6.refs_2_ = f32[88,128]{1,0:T(8,128)S(1)} collective-permute-done((f32[88,128]{1,0:T(8,128)S(1)}, f32[88,128]{1,0:T(8,128)S(1)}, u32[]{:S(2)}, u32[]{:S(2)}) %collective-permute-start.6) | collective-permute-done | bytes 45088 | tf_op jit(solution)/shard_map/ppermute | solution.py:61
  29.1 1.1 %collective-permute-done.5.refs_1_ = f32[88,128]{1,0:T(8,128)S(1)} collective-permute-done((f32[88,128]{1,0:T(8,128)S(1)}, f32[88,128]{1,0:T(8,128)S(1)}, u32[]{:S(2)}, u32[]{:S(2)}) %collective-permute-start.5) | collective-permute-done | bytes 45088 | tf_op jit(solution)/shard_map/ppermute | solution.py:61
  30.2 0.0 copy-done.1
  30.2 1.0 %shard_map.90 = (f32[4,1024]{1,0:T(4,128)S(1)}, f32[4,512]{1,0:T(4,128)S(1)}) custom-call(bf16[64,128]{1,0:T(8,128)(2,1)S(1)} %get-tuple-element.13.query_ref, f32[4,128]{1,0:T(4,128)S(1)} %get-tuple-element.14.scale_ref, bf16[2048,1024]{1,0:T(8,128)(2,1)S(1)} %copy-done.1, f32[88,128]{1,0:T(8,128)S(1)} %get-tuple-element.15.refs_0_, ...), custom_call_target="tpu_custom_call" | custom-call | flops 16777216 | bytes 16777216 | tf_op jit(solution)/shard_map/pallas_call | solution.py:30
  31.2 0.0 collective-permute-start.8
  31.2 0.6 %reshape.16 = bf16[4,2,256]{2,1,0:T(2,128)(2,1)} reshape(bf16[4,512]{1,0:T(4,128)(2,1)S(1)} %convert_element_type.15) | data formatting | bytes 8192 | tf_op jit(solution)/shard_map/reshape | solution.py:318
  31.8 0.6 %collective-permute-done.8 = f32[4,1024]{1,0:T(4,128)S(1)} collective-permute-done((f32[4,1024]{1,0:T(4,128)S(1)}, f32[4,1024]{1,0:T(4,128)S(1)}, u32[]{:S(2)}, u32[]{:S(2)}) %collective-permute-start.8) | collective-permute-done | bytes 16416 | tf_op jit(solution)/shard_map/ppermute | solution.py:316
  32.4 0.6 %fusion.1 = bf16[4,1024]{1,0:T(4,128)(2,1)} fusion(bf16[4,1024]{1,0:T(4,128)(2,1)S(1)} %copy-done.3, f32[4,1024]{1,0:T(4,128)S(1)} %get-tuple-element.16, f32[4,1024]{1,0:T(4,128)S(1)} %collective-permute-done.8), kind=kLoop, calls=%fused_computation.5 | loop fusion | flops 16384 | bytes 49152 | tf_op jit(solution)/shard_map/convert_element_type | solution.py:317
  (4 shorter events, 0.1 us)
Async XLA Ops:
  0.6 2.2 %copy-start = (bf16[1024,2048]{1,0:T(8,128)(2,1)S(1)}, bf16[1024,2048]{1,0:T(8,128)(2,1)}, u32[]{:S(2)}) copy-start(bf16[1024,2048]{1,0:T(8,128)(2,1)} %proj_ref.2) | copy-start | bytes 12582916
  2.8 0.7 %copy-start.2 = (bf16[4,1024]{1,0:T(4,128)(2,1)S(1)}, bf16[4,1024]{1,0:T(4,128)(2,1)}, u32[]{:S(2)}) copy-start(bf16[4,1024]{1,0:T(4,128)(2,1)} %hidden_ref.1) | copy-start | bytes 24580
  3.5 0.7 %copy-start.4 = (f32[1024]{0:T(1024)S(1)}, f32[1024]{0:T(1024)}, u32[]{:S(2)}) copy-start(f32[1024]{0:T(1024)} %param.8) | copy-start | bytes 12292
  4.2 6.4 %copy-start.7 = (bf16[2,4,64,256]{3,2,1,0:T(8,128)(2,1)S(1)}, bf16[2,4,64,256]{3,2,1,0:T(8,128)(2,1)}, u32[]{:S(2)}) copy-start(bf16[2,4,64,256]{3,2,1,0:T(8,128)(2,1)} %cache_ref.1) | copy-start | bytes 786436
  4.9 7.4 %copy-start.8 = (bf16[1024,2,256]{2,1,0:T(2,128)(2,1)S(1)}, bf16[1024,2,256]{2,1,0:T(2,128)(2,1)}, u32[]{:S(2)}) copy-start(bf16[1024,2,256]{2,1,0:T(2,128)(2,1)} %param.10) | copy-start | bytes 3145732
  4.9 7.6 %copy-start.3 = (bf16[4,1024]{1,0:T(4,128)(2,1)S(1)}, bf16[4,1024]{1,0:T(4,128)(2,1)}, u32[]{:S(2)}) copy-start(bf16[4,1024]{1,0:T(4,128)(2,1)} %hidden_ref.1) | copy-start | bytes 24580
  4.9 7.6 %copy-start.5 = (f32[1024]{0:T(1024)S(1)}, f32[1024]{0:T(1024)}, u32[]{:S(2)}) copy-start(f32[1024]{0:T(1024)} %param.8) | copy-start | bytes 12292
  4.9 15.4 %copy-start.6 = (s32[4]{0:T(128)S(1)}, s32[4]{0:T(128)}, u32[]{:S(2)}) copy-start(s32[4]{0:T(128)} %lengths_ref.1) | copy-start | bytes 52
  4.9 7.8 %collective-permute-start.2 = (f32[4,2176]{1,0:T(4,128)S(1)}, f32[4,2176]{1,0:T(4,128)S(1)}, u32[]{:S(2)}, u32[]{:S(2)}) collective-permute-start(f32[4,2176]{1,0:T(4,128)S(1)} %shard_map.86), channel_id=1, source_target_pairs={{0,4},{1,3},{2,6},{3,1},{4,0},{5,7},{6,2},{7,5},{8,12},{9,11},{10,... | collective-permute-start | bytes 104456 | tf_op jit(solution)/shard_map/ppermute | solution.py:61
  8.0 5.9 %collective-permute-start.1 = (f32[4,2176]{1,0:T(4,128)S(1)}, f32[4,2176]{1,0:T(4,128)S(1)}, u32[]{:S(2)}, u32[]{:S(2)}) collective-permute-start(f32[4,2176]{1,0:T(4,128)S(1)} %shard_map.86), channel_id=1, source_target_pairs={{0,12},{1,9},{2,14},{3,11},{4,8},{5,13},{6,10},{7,15},{8,4},{9,1},... | collective-permute-start | bytes 104456 | tf_op jit(solution)/shard_map/ppermute | solution.py:61
  10.5 5.1 %collective-permute-start = (f32[4,2176]{1,0:T(4,128)S(1)}, f32[4,2176]{1,0:T(4,128)S(1)}, u32[]{:S(2)}, u32[]{:S(2)}) collective-permute-start(f32[4,2176]{1,0:T(4,128)S(1)} %shard_map.86), channel_id=1, source_target_pairs={{0,8},{1,11},{2,10},{3,9},{4,12},{5,15},{6,14},{7,13},{8,0},{9,3},... | collective-permute-start | bytes 104456 | tf_op jit(solution)/shard_map/ppermute | solution.py:61
  10.6 19.6 %copy-start.1 = (bf16[2048,1024]{1,0:T(8,128)(2,1)S(1)}, bf16[2048,1024]{1,0:T(8,128)(2,1)}, u32[]{:S(2)}) copy-start(bf16[2048,1024]{1,0:T(8,128)(2,1)} %proj_ref.3) | copy-start | bytes 12582916
  10.6 9.6 %collective-permute-start.4 = (f32[2,4,64,256]{3,2,1,0:T(8,128)S(1)}, f32[2,4,64,256]{3,2,1,0:T(8,128)S(1)}, u32[]{:S(2)}, u32[]{:S(2)}) collective-permute-start(f32[2,4,64,256]{3,2,1,0:T(8,128)S(1)} %shard_map.87.near_ref), channel_id=1, source_target_pairs={{0,2},{1,5},{2,0},{3,7},{4,6},{5,1},{6,4},{7,3},{8,10},{9,13},{10,... | collective-permute-start | bytes 1572872 | tf_op jit(solution)/shard_map/ppermute | solution.py:61
  15.6 5.3 %collective-permute-start.3 = (f32[4,2688]{1,0:T(4,128)S(1)}, f32[4,2688]{1,0:T(4,128)S(1)}, u32[]{:S(2)}, u32[]{:S(2)}) collective-permute-start(f32[4,2688]{1,0:T(4,128)S(1)} %pad_maximum_fusion.mine_ref), channel_id=1, source_target_pairs={{0,2},{1,5},{2,0},{3,7},{4,6},{5,1},{6,4},{7,3},{8,10},{9,13},{10,... | collective-permute-start | bytes 129032 | tf_op jit(solution)/shard_map/ppermute | solution.py:61
  21.3 4.6 %collective-permute-start.7 = (f32[88,128]{1,0:T(8,128)S(1)}, f32[88,128]{1,0:T(8,128)S(1)}, u32[]{:S(2)}, u32[]{:S(2)}) collective-permute-start(f32[88,128]{1,0:T(8,128)S(1)} %get-tuple-element.15.refs_0_), channel_id=1, source_target_pairs={{0,4},{1,3},{2,6},{3,1},{4,0},{5,7},{6,2},{7,5},{8,12},{9,11},{10,... | collective-permute-start | bytes 135176 | tf_op jit(solution)/shard_map/ppermute | solution.py:61
  22.9 6.2 %collective-permute-start.6 = (f32[88,128]{1,0:T(8,128)S(1)}, f32[88,128]{1,0:T(8,128)S(1)}, u32[]{:S(2)}, u32[]{:S(2)}) collective-permute-start(f32[88,128]{1,0:T(8,128)S(1)} %get-tuple-element.15.refs_0_), channel_id=1, source_target_pairs={{0,12},{1,9},{2,14},{3,11},{4,8},{5,13},{6,10},{7,15},{8,4},{9,1},... | collective-permute-start | bytes 135176 | tf_op jit(solution)/shard_map/ppermute | solution.py:61
  25.3 4.9 %collective-permute-start.5 = (f32[88,128]{1,0:T(8,128)S(1)}, f32[88,128]{1,0:T(8,128)S(1)}, u32[]{:S(2)}, u32[]{:S(2)}) collective-permute-start(f32[88,128]{1,0:T(8,128)S(1)} %get-tuple-element.15.refs_0_), channel_id=1, source_target_pairs={{0,8},{1,11},{2,10},{3,9},{4,12},{5,15},{6,14},{7,13},{8,0},{9,3},... | collective-permute-start | bytes 135176 | tf_op jit(solution)/shard_map/ppermute | solution.py:61
  31.2 1.2 %collective-permute-start.8 = (f32[4,1024]{1,0:T(4,128)S(1)}, f32[4,1024]{1,0:T(4,128)S(1)}, u32[]{:S(2)}, u32[]{:S(2)}) collective-permute-start(f32[4,1024]{1,0:T(4,128)S(1)} %get-tuple-element.16), channel_id=1, source_target_pairs={{0,1},{1,0},{2,3},{3,2},{4,5},{5,4},{6,7},{7,6},{8,9},{9,8},{10,11... | collective-permute-start | bytes 49160 | tf_op jit(solution)/shard_map/ppermute | solution.py:316

commit v3 on v2

--- a/solution.py
+++ b/solution.py
@@ -16,11 +16,6 @@
 
 COVER = 16 << 20
 COVER_OPS = 1 << 22
-
-ORDERS = (
-    lambda low, high: (high, low | high, low),
-    lambda low, high: (low | high, high, low),
-)
 
 VMEM = pl.BlockSpec(memory_space=pltpu.VMEM)
 SMEM = pl.BlockSpec(memory_space=pltpu.SMEM)
@@ -48,7 +43,7 @@
     out = []
     while len(bits) > 1:
         low, high, *bits = bits
-        out.append(ORDERS[core % 2](low, high))
+        out.append((low | high, high, low))
     return out + [(bit,) for bit in bits]
 
 
@@ -249,14 +244,7 @@
         core = lax.axis_index("tp")
         return sum(jnp.where(core == c, offset, 0) for c, (offset,) in enumerate(pairs))
 
-    near = call(
-        widen_kernel,
-        [jax.ShapeDtypeStruct(keyval_cache.shape, f32)],
-        [keyval_cache],
-        0,
-        COVER,
-        COVER_OPS,
-    )[0]
+    near = call(widen_kernel, [jax.ShapeDtypeStruct(keyval_cache.shape, f32)], [keyval_cache], 0, COVER, COVER_OPS)[0]
     far = exchange(near, seq, tp, pairs)[0]
 
     first = call(

time: 33.3 us -> 34.3 us (1.030)
  starting transfers between devices: 12.8 us -> 13.5 us
    ppermute x8, starting transfers between devices: 12.8 us -> 13.5 us  [exchange(): got.append(lax.ppermute(value, ('seq', 'tp'), moves))]
where the time goes in v3:
time: 34.3 us; the launch traced here: 34 us
  starting transfers between devices  13.5 us (39%)
  waiting for transfers between devices  11.8 us (34%)
  local copies, waits for them, and re-layouts  4.44 us (13%)
  Pallas kernels  2.71 us (8%)
  between operations  0.72 us (2%)
  other arithmetic  0.65 us (2%)
    ppermute x8, starting transfers between devices, exchange(): got.append(lax.ppermute(value, ('seq', 'tp'), moves))  13.5 us
    ppermute x8, waiting for transfers between devices, exchange(): got.append(lax.ppermute(value, ('seq', 'tp'), moves))  11.2 us
    unnamed x19, local copies, waits for them, and re-layouts  3.83 us
    pallas_call x5, Pallas kernels, call(): pl.pallas_call(kernel, out_shape=outs, in_specs=[SMEM if a.dtype == jnp.i...  2.71 us
  transfers between devices with their start and end apart: 9, of which 7 were waited for; matrix products, arithmetic and copies ran while one was open for 3% of the time, Pallas kernels for 2%

profile of v3, /device:TPU:0, one launch (start us, length us, event | category | flops | bytes accessed | tf_op | source)
XLA Modules:
  0.0 34.0 jit_solution(18262498034734408949)
XLA Ops:
  0.6 0.0 copy-start
  0.6 2.2 %copy-done = bf16[1024,2048]{1,0:T(8,128)(2,1)S(1)} copy-done((bf16[1024,2048]{1,0:T(8,128)(2,1)S(1)}, bf16[1024,2048]{1,0:T(8,128)(2,1)}, u32[]{:S(2)}) %copy-start) | copy-done | bytes 4194328
  2.8 0.0 copy-start.2
  2.8 0.7 %copy-done.2 = bf16[4,1024]{1,0:T(4,128)(2,1)S(1)} copy-done((bf16[4,1024]{1,0:T(4,128)(2,1)S(1)}, bf16[4,1024]{1,0:T(4,128)(2,1)}, u32[]{:S(2)}) %copy-start.2) | copy-done | bytes 8216
  3.5 0.0 copy-start.4
  3.5 0.7 %copy-done.4 = f32[1024]{0:T(1024)S(1)} copy-done((f32[1024]{0:T(1024)S(1)}, f32[1024]{0:T(1024)}, u32[]{:S(2)}) %copy-start.4) | copy-done | bytes 4120
  4.2 0.0 copy-start.7
  4.2 0.6 %shard_map.86 = f32[4,2176]{1,0:T(4,128)S(1)} custom-call(bf16[4,1024]{1,0:T(4,128)(2,1)S(1)} %copy-done.2, f32[1,1024]{1,0:T(1,128)S(1)} %bitcast.4, bf16[1024,2048]{1,0:T(8,128)(2,1)S(1)} %copy-done), custom_call_target="tpu_custom_call" | custom-call | flops 16777216 | bytes 16777216 | tf_op jit(solution)/shard_map/pallas_call | solution.py:25
  4.9 0.0 copy-start.8
  4.9 0.0 copy-start.3
  4.9 0.0 copy-start.5
  4.9 0.0 copy-start.6
  4.9 3.1 %collective-permute-start.2 = (f32[4,2176]{1,0:T(4,128)S(1)}, f32[4,2176]{1,0:T(4,128)S(1)}, u32[]{:S(2)}, u32[]{:S(2)}) collective-permute-start(f32[4,2176]{1,0:T(4,128)S(1)} %shard_map.86), channel_id=1, source_target_pairs={{0,4},{1,3},{2,6},{3,1},{4,0},{5,7},{6,2},{7,5},{8,12},{9,11},{10,... | collective-permute-start | bytes 104456 | tf_op jit(solution)/shard_map/ppermute | solution.py:56
  8.0 2.6 %collective-permute-start.1 = (f32[4,2176]{1,0:T(4,128)S(1)}, f32[4,2176]{1,0:T(4,128)S(1)}, u32[]{:S(2)}, u32[]{:S(2)}) collective-permute-start(f32[4,2176]{1,0:T(4,128)S(1)} %shard_map.86), channel_id=1, source_target_pairs={{0,8},{1,9},{2,10},{3,11},{4,12},{5,13},{6,14},{7,15},{8,0},{9,1},... | collective-permute-start | bytes 104456 | tf_op jit(solution)/shard_map/ppermute | solution.py:56
  10.6 0.0 collective-permute-start
  10.6 0.0 copy-done.7
  10.6 0.0 copy-start.1
  10.6 1.8 %collective-permute-start.4 = (f32[2,4,64,256]{3,2,1,0:T(8,128)S(1)}, f32[2,4,64,256]{3,2,1,0:T(8,128)S(1)}, u32[]{:S(2)}, u32[]{:S(2)}) collective-permute-start(f32[2,4,64,256]{3,2,1,0:T(8,128)S(1)} %shard_map.87.near_ref), channel_id=1, source_target_pairs={{0,2},{1,5},{2,0},{3,7},{4,6},{5,1},{6,4},{7,3},{8,10},{9,13},{10,... | collective-permute-start | bytes 1572872 | tf_op jit(solution)/shard_map/ppermute | solution.py:56
  12.4 0.0 copy-done.8
  12.4 0.2 copy.9
  12.7 0.0 copy-done.3
  12.7 0.0 copy-done.5
  12.7 0.2 fusion.2
  12.9 0.0 collective-permute-done.2
  12.9 0.5 %collective-permute-done.1 = f32[4,2176]{1,0:T(4,128)S(1)} collective-permute-done((f32[4,2176]{1,0:T(4,128)S(1)}, f32[4,2176]{1,0:T(4,128)S(1)}, u32[]{:S(2)}, u32[]{:S(2)}) %collective-permute-start.1) | collective-permute-done | bytes 34848 | tf_op jit(solution)/shard_map/ppermute | solution.py:56
  13.4 3.3 %collective-permute-done = f32[4,2176]{1,0:T(4,128)S(1)} collective-permute-done((f32[4,2176]{1,0:T(4,128)S(1)}, f32[4,2176]{1,0:T(4,128)S(1)}, u32[]{:S(2)}, u32[]{:S(2)}) %collective-permute-start) | collective-permute-done | bytes 34848 | tf_op jit(solution)/shard_map/ppermute | solution.py:56
  16.7 1.6 %collective-permute-start.3 = (f32[4,2688]{1,0:T(4,128)S(1)}, f32[4,2688]{1,0:T(4,128)S(1)}, u32[]{:S(2)}, u32[]{:S(2)}) collective-permute-start(f32[4,2688]{1,0:T(4,128)S(1)} %pad_maximum_fusion.mine_ref), channel_id=1, source_target_pairs={{0,2},{1,5},{2,0},{3,7},{4,6},{5,1},{6,4},{7,3},{8,10},{9,13},{10,... | collective-permute-start | bytes 129032 | tf_op jit(solution)/shard_map/ppermute | solution.py:56
  18.3 1.9 %collective-permute-done.4.far_ref = f32[2,4,64,256]{3,2,1,0:T(8,128)S(1)} collective-permute-done((f32[2,4,64,256]{3,2,1,0:T(8,128)S(1)}, f32[2,4,64,256]{3,2,1,0:T(8,128)S(1)}, u32[]{:S(2)}, u32[]{:S(2)}) %collective-permute-start.4) | collective-permute-done | bytes 524320 | tf_op jit(solution)/shard_map/ppermute | solution.py:56
  20.2 0.0 copy-done.6
  20.2 0.6 %shard_map.88 = (bf16[2,512,128]{2,1,0:T(8,128)(2,1)S(1)}, bf16[2,512,128]{2,1,0:T(8,128)(2,1)S(1)}, f32[64,128]{1,0:T(8,128)S(1)}) custom-call(s32[4]{0:T(128)S(1)} %copy-done.6, f32[2,4,64,256]{3,2,1,0:T(8,128)S(1)} %shard_map.87.near_ref, f32[2,4,64,256]{3,2,1,0:T(8,128)S(1)} %collective-permute-done.4.far_ref), custom_call_target="tpu_custom_call" | custom-call | bytes 524288 | tf_op jit(solution)/shard_map/pallas_call | solution.py:25
  20.8 0.0 collective-permute-done.3.other_ref
  20.8 0.4 %shard_map.89 = (f32[88,128]{1,0:T(8,128)S(1)}, bf16[64,128]{1,0:T(8,128)(2,1)S(1)}, f32[4,128]{1,0:T(4,128)S(1)}) custom-call(f32[4,2688]{1,0:T(4,128)S(1)} %pad_maximum_fusion.mine_ref, f32[4,2688]{1,0:T(4,128)S(1)} %collective-permute-done.3.other_ref, bf16[2,512,128]{2,1,0:T(8,128)(2,1)S(1)} %get-tuple-element.10.keys_ref, ...), custom_call_target="tpu_custom_call" | custom-call | flops 8388608 | bytes 16777216 | tf_op jit(solution)/shard_map/pallas_call | solution.py:25
  21.2 1.0 %collective-permute-start.7 = (f32[88,128]{1,0:T(8,128)S(1)}, f32[88,128]{1,0:T(8,128)S(1)}, u32[]{:S(2)}, u32[]{:S(2)}) collective-permute-start(f32[88,128]{1,0:T(8,128)S(1)} %get-tuple-element.15.refs_0_), channel_id=1, source_target_pairs={{0,4},{1,3},{2,6},{3,1},{4,0},{5,7},{6,2},{7,5},{8,12},{9,11},{10,... | collective-permute-start | bytes 135176 | tf_op jit(solution)/shard_map/ppermute | solution.py:56
  22.3 3.1 %collective-permute-start.6 = (f32[88,128]{1,0:T(8,128)S(1)}, f32[88,128]{1,0:T(8,128)S(1)}, u32[]{:S(2)}, u32[]{:S(2)}) collective-permute-start(f32[88,128]{1,0:T(8,128)S(1)} %get-tuple-element.15.refs_0_), channel_id=1, source_target_pairs={{0,8},{1,9},{2,10},{3,11},{4,12},{5,13},{6,14},{7,15},{8,0},{9,1},... | collective-permute-start | bytes 135176 | tf_op jit(solution)/shard_map/ppermute | solution.py:56
  25.4 0.3 collective-permute-start.5
  25.7 0.1 collective-permute-done.7.refs_3_
  25.8 2.9 %collective-permute-done.6.refs_2_ = f32[88,128]{1,0:T(8,128)S(1)} collective-permute-done((f32[88,128]{1,0:T(8,128)S(1)}, f32[88,128]{1,0:T(8,128)S(1)}, u32[]{:S(2)}, u32[]{:S(2)}) %collective-permute-start.6) | collective-permute-done | bytes 45088 | tf_op jit(solution)/shard_map/ppermute | solution.py:56
  28.7 2.5 %collective-permute-done.5.refs_1_ = f32[88,128]{1,0:T(8,128)S(1)} collective-permute-done((f32[88,128]{1,0:T(8,128)S(1)}, f32[88,128]{1,0:T(8,128)S(1)}, u32[]{:S(2)}, u32[]{:S(2)}) %collective-permute-start.5) | collective-permute-done | bytes 45088 | tf_op jit(solution)/shard_map/ppermute | solution.py:56
  31.2 0.0 copy-done.1
  31.2 1.0 %shard_map.90 = (f32[4,1024]{1,0:T(4,128)S(1)}, f32[4,512]{1,0:T(4,128)S(1)}) custom-call(bf16[64,128]{1,0:T(8,128)(2,1)S(1)} %get-tuple-element.13.query_ref, f32[4,128]{1,0:T(4,128)S(1)} %get-tuple-element.14.scale_ref, bf16[2048,1024]{1,0:T(8,128)(2,1)S(1)} %copy-done.1, f32[88,128]{1,0:T(8,128)S(1)} %get-tuple-element.15.refs_0_, ...), custom_call_target="tpu_custom_call" | custom-call | flops 16777216 | bytes 16777216 | tf_op jit(solution)/shard_map/pallas_call | solution.py:25
  32.2 0.0 collective-permute-start.8
  32.3 0.6 %reshape.16 = bf16[4,2,256]{2,1,0:T(2,128)(2,1)} reshape(bf16[4,512]{1,0:T(4,128)(2,1)S(1)} %convert_element_type.15) | data formatting | bytes 8192 | tf_op jit(solution)/shard_map/reshape | solution.py:306
  32.9 0.6 %collective-permute-done.8 = f32[4,1024]{1,0:T(4,128)S(1)} collective-permute-done((f32[4,1024]{1,0:T(4,128)S(1)}, f32[4,1024]{1,0:T(4,128)S(1)}, u32[]{:S(2)}, u32[]{:S(2)}) %collective-permute-start.8) | collective-permute-done | bytes 16416 | tf_op jit(solution)/shard_map/ppermute | solution.py:304
  33.4 0.6 %fusion.1 = bf16[4,1024]{1,0:T(4,128)(2,1)} fusion(bf16[4,1024]{1,0:T(4,128)(2,1)S(1)} %copy-done.3, f32[4,1024]{1,0:T(4,128)S(1)} %get-tuple-element.16, f32[4,1024]{1,0:T(4,128)S(1)} %collective-permute-done.8), kind=kLoop, calls=%fused_computation.5 | loop fusion | flops 16384 | bytes 49152 | tf_op jit(solution)/shard_map/convert_element_type | solution.py:305
  (4 shorter events, 0.1 us)
Async XLA Ops:
  0.6 2.2 %copy-start = (bf16[1024,2048]{1,0:T(8,128)(2,1)S(1)}, bf16[1024,2048]{1,0:T(8,128)(2,1)}, u32[]{:S(2)}) copy-start(bf16[1024,2048]{1,0:T(8,128)(2,1)} %proj_ref.2) | copy-start | bytes 12582916
  2.8 0.7 %copy-start.2 = (bf16[4,1024]{1,0:T(4,128)(2,1)S(1)}, bf16[4,1024]{1,0:T(4,128)(2,1)}, u32[]{:S(2)}) copy-start(bf16[4,1024]{1,0:T(4,128)(2,1)} %hidden_ref.1) | copy-start | bytes 24580
  3.5 0.7 %copy-start.4 = (f32[1024]{0:T(1024)S(1)}, f32[1024]{0:T(1024)}, u32[]{:S(2)}) copy-start(f32[1024]{0:T(1024)} %param.8) | copy-start | bytes 12292
  4.2 6.4 %copy-start.7 = (bf16[2,4,64,256]{3,2,1,0:T(8,128)(2,1)S(1)}, bf16[2,4,64,256]{3,2,1,0:T(8,128)(2,1)}, u32[]{:S(2)}) copy-start(bf16[2,4,64,256]{3,2,1,0:T(8,128)(2,1)} %cache_ref.1) | copy-start | bytes 786436
  4.9 7.6 %copy-start.8 = (bf16[1024,2,256]{2,1,0:T(2,128)(2,1)S(1)}, bf16[1024,2,256]{2,1,0:T(2,128)(2,1)}, u32[]{:S(2)}) copy-start(bf16[1024,2,256]{2,1,0:T(2,128)(2,1)} %param.10) | copy-start | bytes 3145732
  4.9 7.8 %copy-start.3 = (bf16[4,1024]{1,0:T(4,128)(2,1)S(1)}, bf16[4,1024]{1,0:T(4,128)(2,1)}, u32[]{:S(2)}) copy-start(bf16[4,1024]{1,0:T(4,128)(2,1)} %hidden_ref.1) | copy-start | bytes 24580
  4.9 7.8 %copy-start.5 = (f32[1024]{0:T(1024)S(1)}, f32[1024]{0:T(1024)}, u32[]{:S(2)}) copy-start(f32[1024]{0:T(1024)} %param.8) | copy-start | bytes 12292
  4.9 15.3 %copy-start.6 = (s32[4]{0:T(128)S(1)}, s32[4]{0:T(128)}, u32[]{:S(2)}) copy-start(s32[4]{0:T(128)} %lengths_ref.1) | copy-start | bytes 52
  4.9 8.0 %collective-permute-start.2 = (f32[4,2176]{1,0:T(4,128)S(1)}, f32[4,2176]{1,0:T(4,128)S(1)}, u32[]{:S(2)}, u32[]{:S(2)}) collective-permute-start(f32[4,2176]{1,0:T(4,128)S(1)} %shard_map.86), channel_id=1, source_target_pairs={{0,4},{1,3},{2,6},{3,1},{4,0},{5,7},{6,2},{7,5},{8,12},{9,11},{10,... | collective-permute-start | bytes 104456 | tf_op jit(solution)/shard_map/ppermute | solution.py:56
  8.0 5.4 %collective-permute-start.1 = (f32[4,2176]{1,0:T(4,128)S(1)}, f32[4,2176]{1,0:T(4,128)S(1)}, u32[]{:S(2)}, u32[]{:S(2)}) collective-permute-start(f32[4,2176]{1,0:T(4,128)S(1)} %shard_map.86), channel_id=1, source_target_pairs={{0,8},{1,9},{2,10},{3,11},{4,12},{5,13},{6,14},{7,15},{8,0},{9,1},... | collective-permute-start | bytes 104456 | tf_op jit(solution)/shard_map/ppermute | solution.py:56
  10.6 6.1 %collective-permute-start = (f32[4,2176]{1,0:T(4,128)S(1)}, f32[4,2176]{1,0:T(4,128)S(1)}, u32[]{:S(2)}, u32[]{:S(2)}) collective-permute-start(f32[4,2176]{1,0:T(4,128)S(1)} %shard_map.86), channel_id=1, source_target_pairs={{0,12},{1,11},{2,14},{3,9},{4,8},{5,15},{6,10},{7,13},{8,4},{9,3},... | collective-permute-start | bytes 104456 | tf_op jit(solution)/shard_map/ppermute | solution.py:56
  10.6 20.6 %copy-start.1 = (bf16[2048,1024]{1,0:T(8,128)(2,1)S(1)}, bf16[2048,1024]{1,0:T(8,128)(2,1)}, u32[]{:S(2)}) copy-start(bf16[2048,1024]{1,0:T(8,128)(2,1)} %proj_ref.3) | copy-start | bytes 12582916
  10.6 9.5 %collective-permute-start.4 = (f32[2,4,64,256]{3,2,1,0:T(8,128)S(1)}, f32[2,4,64,256]{3,2,1,0:T(8,128)S(1)}, u32[]{:S(2)}, u32[]{:S(2)}) collective-permute-start(f32[2,4,64,256]{3,2,1,0:T(8,128)S(1)} %shard_map.87.near_ref), channel_id=1, source_target_pairs={{0,2},{1,5},{2,0},{3,7},{4,6},{5,1},{6,4},{7,3},{8,10},{9,13},{10,... | collective-permute-start | bytes 1572872 | tf_op jit(solution)/shard_map/ppermute | solution.py:56
  16.7 4.1 %collective-permute-start.3 = (f32[4,2688]{1,0:T(4,128)S(1)}, f32[4,2688]{1,0:T(4,128)S(1)}, u32[]{:S(2)}, u32[]{:S(2)}) collective-permute-start(f32[4,2688]{1,0:T(4,128)S(1)} %pad_maximum_fusion.mine_ref), channel_id=1, source_target_pairs={{0,2},{1,5},{2,0},{3,7},{4,6},{5,1},{6,4},{7,3},{8,10},{9,13},{10,... | collective-permute-start | bytes 129032 | tf_op jit(solution)/shard_map/ppermute | solution.py:56
  21.2 4.6 %collective-permute-start.7 = (f32[88,128]{1,0:T(8,128)S(1)}, f32[88,128]{1,0:T(8,128)S(1)}, u32[]{:S(2)}, u32[]{:S(2)}) collective-permute-start(f32[88,128]{1,0:T(8,128)S(1)} %get-tuple-element.15.refs_0_), channel_id=1, source_target_pairs={{0,4},{1,3},{2,6},{3,1},{4,0},{5,7},{6,2},{7,5},{8,12},{9,11},{10,... | collective-permute-start | bytes 135176 | tf_op jit(solution)/shard_map/ppermute | solution.py:56
  22.3 6.5 %collective-permute-start.6 = (f32[88,128]{1,0:T(8,128)S(1)}, f32[88,128]{1,0:T(8,128)S(1)}, u32[]{:S(2)}, u32[]{:S(2)}) collective-permute-start(f32[88,128]{1,0:T(8,128)S(1)} %get-tuple-element.15.refs_0_), channel_id=1, source_target_pairs={{0,8},{1,9},{2,10},{3,11},{4,12},{5,13},{6,14},{7,15},{8,0},{9,1},... | collective-permute-start | bytes 135176 | tf_op jit(solution)/shard_map/ppermute | solution.py:56
  25.4 5.8 %collective-permute-start.5 = (f32[88,128]{1,0:T(8,128)S(1)}, f32[88,128]{1,0:T(8,128)S(1)}, u32[]{:S(2)}, u32[]{:S(2)}) collective-permute-start(f32[88,128]{1,0:T(8,128)S(1)} %get-tuple-element.15.refs_0_), channel_id=1, source_target_pairs={{0,12},{1,11},{2,14},{3,9},{4,8},{5,15},{6,10},{7,13},{8,4},{9,3},... | collective-permute-start | bytes 135176 | tf_op jit(solution)/shard_map/ppermute | solution.py:56
  32.2 1.2 %collective-permute-start.8 = (f32[4,1024]{1,0:T(4,128)S(1)}, f32[4,1024]{1,0:T(4,128)S(1)}, u32[]{:S(2)}, u32[]{:S(2)}) collective-permute-start(f32[4,1024]{1,0:T(4,128)S(1)} %get-tuple-element.16), channel_id=1, source_target_pairs={{0,1},{1,0},{2,3},{3,2},{4,5},{5,4},{6,7},{7,6},{8,9},{9,8},{10,11... | collective-permute-start | bytes 49160 | tf_op jit(solution)/shard_map/ppermute | solution.py:304

commit v4 on v3

--- a/solution.py
+++ b/solution.py
@@ -45,6 +45,13 @@
         low, high, *bits = bits
         out.append((low | high, high, low))
     return out + [(bit,) for bit in bits]
+
+
+def reorder(offsets, turn):
+    return [
+        (o[1], o[0], *o[2:]) if len(o) > 1 and core % 2 == turn else o
+        for core, o in enumerate(offsets)
+    ]
 
 
 def exchange(value, seq, tp, offsets):
@@ -168,27 +175,25 @@
         )
 
 
-def unpack(packed, split):
-    pair = jnp.transpose(packed[split : split + 8])
-    return packed[:split], pair[:split, 0:1], pair[:split, 1:2], packed[split + 8 :]
-
-
-def merge(parts):
-    best = functools.reduce(jnp.maximum, [p[1] for p in parts])
-    factors = [jnp.exp(p[1] - best) for p in parts]
-    gathered = sum(f * p[0] for f, p in zip(factors, parts))
-    total = sum(f * p[2] for f, p in zip(factors, parts))
-    return gathered, best, total, sum(p[3] for p in parts)
+def merge(packed, split):
+    best = functools.reduce(jnp.maximum, [p[split : split + 1] for p in packed])
+    factors = [jnp.exp(p[split : split + 1] - best) for p in packed]
+    total = sum(f * p[split + 1 : split + 2] for f, p in zip(factors, packed))
+    row = lax.broadcasted_iota(jnp.int32, (8, HEAD_DIM), 0)
+    stats = jnp.where(row == 0, best, jnp.where(row == 1, total, 0.0))
+    for place, factor in enumerate(factors):
+        stats = jnp.where(row == place + 2, factor, stats)
+    columns = jnp.transpose(stats)[:split]
+    gathered = sum(columns[:, 2 + i : 3 + i] * p[:split] for i, p in enumerate(packed))
+    keyval = sum(p[split + 8 :] for p in packed)
+    return gathered, columns[:, 0:1], columns[:, 1:2], keyval, jnp.where(row < 2, stats, 0.0)
 
 
 def merge_kernel(split, *refs):
-    gathered, best, total, keyval = merge([unpack(ref[...], split) for ref in refs[:-1]])
     packed_ref = refs[-1]
+    gathered, _, _, keyval, stats = merge([ref[...] for ref in refs[:-1]], split)
     packed_ref[:split, :] = gathered
-    column = lax.broadcasted_iota(jnp.int32, (split, HEAD_DIM), 1)
-    pair = jnp.where(column == 0, best, jnp.where(column == 1, total, 0.0))
-    pair = jnp.concatenate([pair, jnp.zeros((HEAD_DIM - split, HEAD_DIM), jnp.float32)], axis=0)
-    packed_ref[split : split + 8, :] = jnp.transpose(pair)[:8]
+    packed_ref[split : split + 8, :] = stats
     packed_ref[split + 8 :, :] = keyval
 
 
@@ -196,7 +201,7 @@
     packed, (out_ref, new_ref) = refs[:parts], refs[parts:]
     split = query_ref.shape[0]
     rows = scale_ref.shape[0]
-    gathered, best, total, keyval = merge([unpack(ref[...], split) for ref in packed])
+    gathered, best, total, keyval, _ = merge([ref[...] for ref in packed], split)
     kv_heads = keyval.shape[0] // rows // 2
     group = split // rows // kv_heads
     new = (keyval * jnp.concatenate([scale_ref[...]] * (2 * kv_heads), axis=0)).astype(jnp.bfloat16)
@@ -255,7 +260,7 @@
         COVER,
     )[0]
     for offsets in rounds:
-        for other in exchange(first, seq, tp, offsets):
+        for other in exchange(first, seq, tp, reorder(offsets, 0)):
             first = first + other
     scaled = (one_float * norm_gain).astype(jnp.bfloat16)
     keyval_part = jnp.dot(
@@ -285,9 +290,10 @@
         [first, second, keys, values, live],
         16 * split * keyval_cache.shape[2] * HEAD_DIM,
         COVER,
+        COVER_OPS,
     )
     for place, offsets in enumerate(rounds):
-        parts = [packed] + exchange(packed, seq, tp, offsets)
+        parts = [packed] + exchange(packed, seq, tp, reorder(offsets, 1))
         if place < len(rounds) - 1:
             packed = call(functools.partial(merge_kernel, split), [pack], parts, 0, COVER)[0]
     term, new_keyval = call(

time: 34.3 us -> 33.4 us (0.974)
  waiting for transfers between devices: 11.8 us -> 11.1 us
    ppermute x8, waiting for transfers between devices: 11.2 us -> 10.5 us  [exchange(): got.append(lax.ppermute(value, ('seq', 'tp'), moves))]
where the time goes in v4:
time: 33.4 us; the launch traced here: 33.1 us
  starting transfers between devices  13.3 us (40%)
  waiting for transfers between devices  11.1 us (33%)
  local copies, waits for them, and re-layouts  4.43 us (13%)
  Pallas kernels  2.7 us (8%)
  between operations  0.73 us (2%)
  other arithmetic  0.64 us (2%)
    ppermute x8, starting transfers between devices, exchange(): got.append(lax.ppermute(value, ('seq', 'tp'), moves))  13.3 us
    ppermute x8, waiting for transfers between devices, exchange(): got.append(lax.ppermute(value, ('seq', 'tp'), moves))  10.5 us
    unnamed x19, local copies, waits for them, and re-layouts  3.83 us
    pallas_call x5, Pallas kernels, call(): pl.pallas_call(kernel, out_shape=outs, in_specs=[SMEM if a.dtype == jnp.i...  2.7 us
  transfers between devices with their start and end apart: 9, of which 7 were waited for; matrix products, arithmetic and copies ran while one was open for 3% of the time, Pallas kernels for 2%

profile of v4, /device:TPU:0, one launch (start us, length us, event | category | flops | bytes accessed | tf_op | source)
XLA Modules:
  0.0 33.1 jit_solution(12856926676105601869)
XLA Ops:
  0.6 0.0 copy-start
  0.6 2.2 %copy-done = bf16[1024,2048]{1,0:T(8,128)(2,1)S(1)} copy-done((bf16[1024,2048]{1,0:T(8,128)(2,1)S(1)}, bf16[1024,2048]{1,0:T(8,128)(2,1)}, u32[]{:S(2)}) %copy-start) | copy-done | bytes 4194328
  2.8 0.0 copy-start.2
  2.8 0.7 %copy-done.2 = bf16[4,1024]{1,0:T(4,128)(2,1)S(1)} copy-done((bf16[4,1024]{1,0:T(4,128)(2,1)S(1)}, bf16[4,1024]{1,0:T(4,128)(2,1)}, u32[]{:S(2)}) %copy-start.2) | copy-done | bytes 8216
  3.5 0.0 copy-start.4
  3.5 0.7 %copy-done.4 = f32[1024]{0:T(1024)S(1)} copy-done((f32[1024]{0:T(1024)S(1)}, f32[1024]{0:T(1024)}, u32[]{:S(2)}) %copy-start.4) | copy-done | bytes 4120
  4.2 0.0 copy-start.7
  4.2 0.6 %shard_map.86 = f32[4,2176]{1,0:T(4,128)S(1)} custom-call(bf16[4,1024]{1,0:T(4,128)(2,1)S(1)} %copy-done.2, f32[1,1024]{1,0:T(1,128)S(1)} %bitcast.4, bf16[1024,2048]{1,0:T(8,128)(2,1)S(1)} %copy-done), custom_call_target="tpu_custom_call" | custom-call | flops 16777216 | bytes 16777216 | tf_op jit(solution)/shard_map/pallas_call | solution.py:25
  4.9 0.0 copy-start.8
  4.9 0.0 copy-start.3
  4.9 0.0 copy-start.5
  4.9 0.0 copy-start.6
  4.9 3.1 %collective-permute-start.2 = (f32[4,2176]{1,0:T(4,128)S(1)}, f32[4,2176]{1,0:T(4,128)S(1)}, u32[]{:S(2)}, u32[]{:S(2)}) collective-permute-start(f32[4,2176]{1,0:T(4,128)S(1)} %shard_map.86), channel_id=1, source_target_pairs={{0,4},{1,3},{2,6},{3,1},{4,0},{5,7},{6,2},{7,5},{8,12},{9,11},{10,... | collective-permute-start | bytes 104456 | tf_op jit(solution)/shard_map/ppermute | solution.py:63
  8.0 2.5 %collective-permute-start.1 = (f32[4,2176]{1,0:T(4,128)S(1)}, f32[4,2176]{1,0:T(4,128)S(1)}, u32[]{:S(2)}, u32[]{:S(2)}) collective-permute-start(f32[4,2176]{1,0:T(4,128)S(1)} %shard_map.86), channel_id=1, source_target_pairs={{0,12},{1,9},{2,14},{3,11},{4,8},{5,13},{6,10},{7,15},{8,4},{9,1},... | collective-permute-start | bytes 104456 | tf_op jit(solution)/shard_map/ppermute | solution.py:63
  10.5 0.1 collective-permute-start
  10.6 0.0 copy-done.7
  10.6 1.6 %collective-permute-start.4 = (f32[2,4,64,256]{3,2,1,0:T(8,128)S(1)}, f32[2,4,64,256]{3,2,1,0:T(8,128)S(1)}, u32[]{:S(2)}, u32[]{:S(2)}) collective-permute-start(f32[2,4,64,256]{3,2,1,0:T(8,128)S(1)} %shard_map.87.near_ref), channel_id=1, source_target_pairs={{0,2},{1,5},{2,0},{3,7},{4,6},{5,1},{6,4},{7,3},{8,10},{9,13},{10,... | collective-permute-start | bytes 1572872 | tf_op jit(solution)/shard_map/ppermute | solution.py:63
  12.2 0.0 copy-done.8
  12.2 0.2 copy.9
  12.4 0.0 copy-done.3
  12.4 0.0 copy-done.5
  12.5 0.2 fusion.2
  12.7 0.0 collective-permute-done.2
  12.7 1.2 %collective-permute-done.1 = f32[4,2176]{1,0:T(4,128)S(1)} collective-permute-done((f32[4,2176]{1,0:T(4,128)S(1)}, f32[4,2176]{1,0:T(4,128)S(1)}, u32[]{:S(2)}, u32[]{:S(2)}) %collective-permute-start.1) | collective-permute-done | bytes 34848 | tf_op jit(solution)/shard_map/ppermute | solution.py:63
  13.9 1.6 %collective-permute-done = f32[4,2176]{1,0:T(4,128)S(1)} collective-permute-done((f32[4,2176]{1,0:T(4,128)S(1)}, f32[4,2176]{1,0:T(4,128)S(1)}, u32[]{:S(2)}, u32[]{:S(2)}) %collective-permute-start) | collective-permute-done | bytes 34848 | tf_op jit(solution)/shard_map/ppermute | solution.py:63
  15.6 1.6 %collective-permute-start.3 = (f32[4,2688]{1,0:T(4,128)S(1)}, f32[4,2688]{1,0:T(4,128)S(1)}, u32[]{:S(2)}, u32[]{:S(2)}) collective-permute-start(f32[4,2688]{1,0:T(4,128)S(1)} %pad_maximum_fusion.mine_ref), channel_id=1, source_target_pairs={{0,2},{1,5},{2,0},{3,7},{4,6},{5,1},{6,4},{7,3},{8,10},{9,13},{10,... | collective-permute-start | bytes 129032 | tf_op jit(solution)/shard_map/ppermute | solution.py:63
  17.2 3.1 %collective-permute-done.4.far_ref = f32[2,4,64,256]{3,2,1,0:T(8,128)S(1)} collective-permute-done((f32[2,4,64,256]{3,2,1,0:T(8,128)S(1)}, f32[2,4,64,256]{3,2,1,0:T(8,128)S(1)}, u32[]{:S(2)}, u32[]{:S(2)}) %collective-permute-start.4) | collective-permute-done | bytes 524320 | tf_op jit(solution)/shard_map/ppermute | solution.py:63
  20.2 0.0 copy-done.6
  20.2 0.6 %shard_map.88 = (bf16[2,512,128]{2,1,0:T(8,128)(2,1)S(1)}, bf16[2,512,128]{2,1,0:T(8,128)(2,1)S(1)}, f32[64,128]{1,0:T(8,128)S(1)}) custom-call(s32[4]{0:T(128)S(1)} %copy-done.6, f32[2,4,64,256]{3,2,1,0:T(8,128)S(1)} %shard_map.87.near_ref, f32[2,4,64,256]{3,2,1,0:T(8,128)S(1)} %collective-permute-done.4.far_ref), custom_call_target="tpu_custom_call" | custom-call | bytes 524288 | tf_op jit(solution)/shard_map/pallas_call | solution.py:25
  20.9 0.0 copy-start.1
  20.9 0.0 collective-permute-done.3.other_ref
  20.9 0.4 %shard_map.89 = (f32[88,128]{1,0:T(8,128)S(1)}, bf16[64,128]{1,0:T(8,128)(2,1)S(1)}, f32[4,128]{1,0:T(4,128)S(1)}) custom-call(f32[4,2688]{1,0:T(4,128)S(1)} %pad_maximum_fusion.mine_ref, f32[4,2688]{1,0:T(4,128)S(1)} %collective-permute-done.3.other_ref, bf16[2,512,128]{2,1,0:T(8,128)(2,1)S(1)} %get-tuple-element.10.keys_ref, ...), custom_call_target="tpu_custom_call" | custom-call | flops 8388608 | bytes 16777216 | tf_op jit(solution)/shard_map/pallas_call | solution.py:25
  21.3 1.6 %collective-permute-start.7 = (f32[88,128]{1,0:T(8,128)S(1)}, f32[88,128]{1,0:T(8,128)S(1)}, u32[]{:S(2)}, u32[]{:S(2)}) collective-permute-start(f32[88,128]{1,0:T(8,128)S(1)} %get-tuple-element.15.refs_0_), channel_id=1, source_target_pairs={{0,4},{1,3},{2,6},{3,1},{4,0},{5,7},{6,2},{7,5},{8,12},{9,11},{10,... | collective-permute-start | bytes 135176 | tf_op jit(solution)/shard_map/ppermute | solution.py:63
  22.9 1.6 %collective-permute-start.6 = (f32[88,128]{1,0:T(8,128)S(1)}, f32[88,128]{1,0:T(8,128)S(1)}, u32[]{:S(2)}, u32[]{:S(2)}) collective-permute-start(f32[88,128]{1,0:T(8,128)S(1)} %get-tuple-element.15.refs_0_), channel_id=1, source_target_pairs={{0,8},{1,11},{2,10},{3,9},{4,12},{5,15},{6,14},{7,13},{8,0},{9,3},... | collective-permute-start | bytes 135176 | tf_op jit(solution)/shard_map/ppermute | solution.py:63
  24.5 1.3 %collective-permute-start.5 = (f32[88,128]{1,0:T(8,128)S(1)}, f32[88,128]{1,0:T(8,128)S(1)}, u32[]{:S(2)}, u32[]{:S(2)}) collective-permute-start(f32[88,128]{1,0:T(8,128)S(1)} %get-tuple-element.15.refs_0_), channel_id=1, source_target_pairs={{0,12},{1,9},{2,14},{3,11},{4,8},{5,13},{6,10},{7,15},{8,4},{9,1},... | collective-permute-start | bytes 135176 | tf_op jit(solution)/shard_map/ppermute | solution.py:63
  25.8 0.1 collective-permute-done.7.refs_3_
  25.9 2.4 %collective-permute-done.6.refs_2_ = f32[88,128]{1,0:T(8,128)S(1)} collective-permute-done((f32[88,128]{1,0:T(8,128)S(1)}, f32[88,128]{1,0:T(8,128)S(1)}, u32[]{:S(2)}, u32[]{:S(2)}) %collective-permute-start.6) | collective-permute-done | bytes 45088 | tf_op jit(solution)/shard_map/ppermute | solution.py:63
  28.3 2.1 %collective-permute-done.5.refs_1_ = f32[88,128]{1,0:T(8,128)S(1)} collective-permute-done((f32[88,128]{1,0:T(8,128)S(1)}, f32[88,128]{1,0:T(8,128)S(1)}, u32[]{:S(2)}, u32[]{:S(2)}) %collective-permute-start.5) | collective-permute-done | bytes 45088 | tf_op jit(solution)/shard_map/ppermute | solution.py:63
  30.3 0.0 copy-done.1
  30.3 1.0 %shard_map.90 = (f32[4,1024]{1,0:T(4,128)S(1)}, f32[4,512]{1,0:T(4,128)S(1)}) custom-call(bf16[64,128]{1,0:T(8,128)(2,1)S(1)} %get-tuple-element.13.query_ref, f32[4,128]{1,0:T(4,128)S(1)} %get-tuple-element.14.scale_ref, bf16[2048,1024]{1,0:T(8,128)(2,1)S(1)} %copy-done.1, f32[88,128]{1,0:T(8,128)S(1)} %get-tuple-element.15.refs_0_, ...), custom_call_target="tpu_custom_call" | custom-call | flops 16777216 | bytes 16777216 | tf_op jit(solution)/shard_map/pallas_call | solution.py:25
  31.3 0.0 collective-permute-start.8
  31.3 0.6 %reshape.16 = bf16[4,2,256]{2,1,0:T(2,128)(2,1)} reshape(bf16[4,512]{1,0:T(4,128)(2,1)S(1)} %convert_element_type.15) | data formatting | bytes 8192 | tf_op jit(solution)/shard_map/reshape | solution.py:312
  32.0 0.6 %collective-permute-done.8 = f32[4,1024]{1,0:T(4,128)S(1)} collective-permute-done((f32[4,1024]{1,0:T(4,128)S(1)}, f32[4,1024]{1,0:T(4,128)S(1)}, u32[]{:S(2)}, u32[]{:S(2)}) %collective-permute-start.8) | collective-permute-done | bytes 16416 | tf_op jit(solution)/shard_map/ppermute | solution.py:310
  32.5 0.6 %fusion.1 = bf16[4,1024]{1,0:T(4,128)(2,1)} fusion(bf16[4,1024]{1,0:T(4,128)(2,1)S(1)} %copy-done.3, f32[4,1024]{1,0:T(4,128)S(1)} %get-tuple-element.16, f32[4,1024]{1,0:T(4,128)S(1)} %collective-permute-done.8), kind=kLoop, calls=%fused_computation.5 | loop fusion | flops 16384 | bytes 49152 | tf_op jit(solution)/shard_map/convert_element_type | solution.py:311
  (4 shorter events, 0.1 us)
Async XLA Ops:
  0.6 2.2 %copy-start = (bf16[1024,2048]{1,0:T(8,128)(2,1)S(1)}, bf16[1024,2048]{1,0:T(8,128)(2,1)}, u32[]{:S(2)}) copy-start(bf16[1024,2048]{1,0:T(8,128)(2,1)} %proj_ref.2) | copy-start | bytes 12582916
  2.8 0.7 %copy-start.2 = (bf16[4,1024]{1,0:T(4,128)(2,1)S(1)}, bf16[4,1024]{1,0:T(4,128)(2,1)}, u32[]{:S(2)}) copy-start(bf16[4,1024]{1,0:T(4,128)(2,1)} %hidden_ref.1) | copy-start | bytes 24580
  3.5 0.7 %copy-start.4 = (f32[1024]{0:T(1024)S(1)}, f32[1024]{0:T(1024)}, u32[]{:S(2)}) copy-start(f32[1024]{0:T(1024)} %param.8) | copy-start | bytes 12292
  4.2 6.4 %copy-start.7 = (bf16[2,4,64,256]{3,2,1,0:T(8,128)(2,1)S(1)}, bf16[2,4,64,256]{3,2,1,0:T(8,128)(2,1)}, u32[]{:S(2)}) copy-start(bf16[2,4,64,256]{3,2,1,0:T(8,128)(2,1)} %cache_ref.1) | copy-start | bytes 786436
  4.9 7.3 %copy-start.8 = (bf16[1024,2,256]{2,1,0:T(2,128)(2,1)S(1)}, bf16[1024,2,256]{2,1,0:T(2,128)(2,1)}, u32[]{:S(2)}) copy-start(bf16[1024,2,256]{2,1,0:T(2,128)(2,1)} %param.10) | copy-start | bytes 3145732
  4.9 7.6 %copy-start.3 = (bf16[4,1024]{1,0:T(4,128)(2,1)S(1)}, bf16[4,1024]{1,0:T(4,128)(2,1)}, u32[]{:S(2)}) copy-start(bf16[4,1024]{1,0:T(4,128)(2,1)} %hidden_ref.1) | copy-start | bytes 24580
  4.9 7.6 %copy-start.5 = (f32[1024]{0:T(1024)S(1)}, f32[1024]{0:T(1024)}, u32[]{:S(2)}) copy-start(f32[1024]{0:T(1024)} %param.8) | copy-start | bytes 12292
  4.9 15.4 %copy-start.6 = (s32[4]{0:T(128)S(1)}, s32[4]{0:T(128)}, u32[]{:S(2)}) copy-start(s32[4]{0:T(128)} %lengths_ref.1) | copy-start | bytes 52
  4.9 7.8 %collective-permute-start.2 = (f32[4,2176]{1,0:T(4,128)S(1)}, f32[4,2176]{1,0:T(4,128)S(1)}, u32[]{:S(2)}, u32[]{:S(2)}) collective-permute-start(f32[4,2176]{1,0:T(4,128)S(1)} %shard_map.86), channel_id=1, source_target_pairs={{0,4},{1,3},{2,6},{3,1},{4,0},{5,7},{6,2},{7,5},{8,12},{9,11},{10,... | collective-permute-start | bytes 104456 | tf_op jit(solution)/shard_map/ppermute | solution.py:63
  8.0 5.9 %collective-permute-start.1 = (f32[4,2176]{1,0:T(4,128)S(1)}, f32[4,2176]{1,0:T(4,128)S(1)}, u32[]{:S(2)}, u32[]{:S(2)}) collective-permute-start(f32[4,2176]{1,0:T(4,128)S(1)} %shard_map.86), channel_id=1, source_target_pairs={{0,12},{1,9},{2,14},{3,11},{4,8},{5,13},{6,10},{7,15},{8,4},{9,1},... | collective-permute-start | bytes 104456 | tf_op jit(solution)/shard_map/ppermute | solution.py:63
  10.5 5.1 %collective-permute-start = (f32[4,2176]{1,0:T(4,128)S(1)}, f32[4,2176]{1,0:T(4,128)S(1)}, u32[]{:S(2)}, u32[]{:S(2)}) collective-permute-start(f32[4,2176]{1,0:T(4,128)S(1)} %shard_map.86), channel_id=1, source_target_pairs={{0,8},{1,11},{2,10},{3,9},{4,12},{5,15},{6,14},{7,13},{8,0},{9,3},... | collective-permute-start | bytes 104456 | tf_op jit(solution)/shard_map/ppermute | solution.py:63
  10.6 9.6 %collective-permute-start.4 = (f32[2,4,64,256]{3,2,1,0:T(8,128)S(1)}, f32[2,4,64,256]{3,2,1,0:T(8,128)S(1)}, u32[]{:S(2)}, u32[]{:S(2)}) collective-permute-start(f32[2,4,64,256]{3,2,1,0:T(8,128)S(1)} %shard_map.87.near_ref), channel_id=1, source_target_pairs={{0,2},{1,5},{2,0},{3,7},{4,6},{5,1},{6,4},{7,3},{8,10},{9,13},{10,... | collective-permute-start | bytes 1572872 | tf_op jit(solution)/shard_map/ppermute | solution.py:63
  15.6 5.3 %collective-permute-start.3 = (f32[4,2688]{1,0:T(4,128)S(1)}, f32[4,2688]{1,0:T(4,128)S(1)}, u32[]{:S(2)}, u32[]{:S(2)}) collective-permute-start(f32[4,2688]{1,0:T(4,128)S(1)} %pad_maximum_fusion.mine_ref), channel_id=1, source_target_pairs={{0,2},{1,5},{2,0},{3,7},{4,6},{5,1},{6,4},{7,3},{8,10},{9,13},{10,... | collective-permute-start | bytes 129032 | tf_op jit(solution)/shard_map/ppermute | solution.py:63
  20.9 9.5 %copy-start.1 = (bf16[2048,1024]{1,0:T(8,128)(2,1)S(1)}, bf16[2048,1024]{1,0:T(8,128)(2,1)}, u32[]{:S(2)}) copy-start(bf16[2048,1024]{1,0:T(8,128)(2,1)} %proj_ref.3) | copy-start | bytes 12582916
  21.3 4.6 %collective-permute-start.7 = (f32[88,128]{1,0:T(8,128)S(1)}, f32[88,128]{1,0:T(8,128)S(1)}, u32[]{:S(2)}, u32[]{:S(2)}) collective-permute-start(f32[88,128]{1,0:T(8,128)S(1)} %get-tuple-element.15.refs_0_), channel_id=1, source_target_pairs={{0,4},{1,3},{2,6},{3,1},{4,0},{5,7},{6,2},{7,5},{8,12},{9,11},{10,... | collective-permute-start | bytes 135176 | tf_op jit(solution)/shard_map/ppermute | solution.py:63
  22.9 5.4 %collective-permute-start.6 = (f32[88,128]{1,0:T(8,128)S(1)}, f32[88,128]{1,0:T(8,128)S(1)}, u32[]{:S(2)}, u32[]{:S(2)}) collective-permute-start(f32[88,128]{1,0:T(8,128)S(1)} %get-tuple-element.15.refs_0_), channel_id=1, source_target_pairs={{0,8},{1,11},{2,10},{3,9},{4,12},{5,15},{6,14},{7,13},{8,0},{9,3},... | collective-permute-start | bytes 135176 | tf_op jit(solution)/shard_map/ppermute | solution.py:63
  24.5 5.8 %collective-permute-start.5 = (f32[88,128]{1,0:T(8,128)S(1)}, f32[88,128]{1,0:T(8,128)S(1)}, u32[]{:S(2)}, u32[]{:S(2)}) collective-permute-start(f32[88,128]{1,0:T(8,128)S(1)} %get-tuple-element.15.refs_0_), channel_id=1, source_target_pairs={{0,12},{1,9},{2,14},{3,11},{4,8},{5,13},{6,10},{7,15},{8,4},{9,1},... | collective-permute-start | bytes 135176 | tf_op jit(solution)/shard_map/ppermute | solution.py:63
  31.3 1.2 %collective-permute-start.8 = (f32[4,1024]{1,0:T(4,128)S(1)}, f32[4,1024]{1,0:T(4,128)S(1)}, u32[]{:S(2)}, u32[]{:S(2)}) collective-permute-start(f32[4,1024]{1,0:T(4,128)S(1)} %get-tuple-element.16), channel_id=1, source_target_pairs={{0,1},{1,0},{2,3},{3,2},{4,5},{5,4},{6,7},{7,6},{8,9},{9,8},{10,11... | collective-permute-start | bytes 49160 | tf_op jit(solution)/shard_map/ppermute | solution.py:310
